TPU v7x, 128 devices: a whole 4x4x4 slice. The times are simulated.
128 devices in a mesh: gx: 4 (over z), gy: 32 (over y, x, core).
Axes of the slice: x: 4, y: 4, z: 4, core: 2. Of those that a mesh axis runs over, the one named last changes fastest.
Arguments:
- positions: float32 [3, 262144], P(None, ('gx', 'gy')), may hold values from -1 to 1
- normals: float32 [3, 262144], P(None, ('gx', 'gy')), may hold values from -4 to 4
- emission: float32 [16, 262144], P(None, ('gx', 'gy')), may hold values from 0.05 to 2
- material: int32 [262144], P(('gx', 'gy')), may hold values from 0 to 7
- area_level: int32 [262144], P(('gx', 'gy')), may hold values from 0 to 7
- reflect_table: float32 [8, 16], replicated, may hold values from 0.1 to 0.9
- area_table: float32 [8], replicated, may hold values from 0.002 to 0.008
- pair_slots: int32 [128, 128, 2, 2], P(('gx', 'gy')), may hold values from -1 to 7, as said below
Outputs:
- radiosity: float32 [16, 262144], P(None, ('gx', 'gy'))
Inputs may be any that keep to these rules, and one draw needn't show every extreme that they name: `pair_slots`: in slot [q, p, c], a row entry is -1 exactly when its column entry is -1; the non-empty slots of one [q, p] come first, at most 2 of them, and the slot group [q, q] is always full. No unordered pair of blocks occurs twice, and a slot never names the same block twice.
All inputs are finite; a program needn't handle non-finite values.
Results may differ from a plain program's by a relative error of at most 0.0017.
Values may be sent and summed in bfloat16 or wider, within the bound.
A program may use at most 64 MiB of HBM per device.

v0:
```python
import math

import jax
import jax.numpy as jnp
from jax import lax
from jax.sharding import PartitionSpec as P

BANDS = 16
BLK = 256
CAP = 2
ITERS = 2


def view_tile(row_geo, col_geo):
    delta = [col_geo[k][None, :] - row_geo[k][:, None] for k in range(3)]
    squared = delta[0] * delta[0] + delta[1] * delta[1] + delta[2] * delta[2]
    facing = jnp.maximum(
        row_geo[3][:, None] * delta[0]
        + row_geo[4][:, None] * delta[1]
        + row_geo[5][:, None] * delta[2],
        0.0,
    )
    seen = jnp.maximum(
        -(
            col_geo[3][None, :] * delta[0]
            + col_geo[4][None, :] * delta[1]
            + col_geo[5][None, :] * delta[2]
        ),
        0.0,
    )
    mean_area = 0.5 * (row_geo[6][:, None] + col_geo[6][None, :])
    return facing * seen / ((squared + mean_area) * (math.pi * squared + mean_area))


def move_flux(blocks):
    return lax.all_to_all(blocks, ("gx", "gy"), split_axis=0, concat_axis=0, tiled=True)


def move_back(blocks):
    return lax.all_to_all(
        blocks.astype(jnp.bfloat16), ("gx", "gy"), split_axis=0, concat_axis=0, tiled=True
    ).astype(blocks.dtype)


def per_device(
    positions, normals, emission, material, area_level, reflect_table, area_table, pair_slots
):
    patches = positions.shape[1]
    nblocks = patches // BLK
    level_hot = (
        area_level[None, :] == jnp.arange(area_table.shape[0], dtype=jnp.int32)[:, None]
    ).astype(jnp.float32)
    area = jnp.sum(level_hot * area_table[:, None], axis=0)
    kind_hot = (
        material[None, :] == jnp.arange(reflect_table.shape[0], dtype=jnp.int32)[:, None]
    ).astype(jnp.float32)
    reflect = jnp.dot(jnp.transpose(reflect_table), kind_hot, precision=lax.Precision.HIGHEST)
    geometry = jnp.concatenate([positions, normals, area[None, :]], axis=0)
    geo_blocks = jnp.transpose(geometry.reshape(7, nblocks, BLK), (1, 0, 2))
    slots_here = pair_slots[0]
    peers = slots_here.shape[0]
    width = peers * CAP
    row_local = slots_here[..., 0]
    col_local = slots_here[..., 1]
    usable = (row_local >= 0).astype(jnp.float32)
    row_block = jnp.maximum(row_local, 0)
    served = lax.all_to_all(col_local, ("gx", "gy"), split_axis=0, concat_axis=0, tiled=True)
    served_ok = (served >= 0).astype(jnp.float32)
    served_block = jnp.maximum(served, 0)
    local_geo = geo_blocks[row_block]
    requested_geo = geo_blocks[served_block]
    remote_geo = lax.all_to_all(
        requested_geo, ("gx", "gy"), split_axis=0, concat_axis=0, tiled=True
    )
    block_ids = jnp.arange(nblocks, dtype=jnp.int32)[:, None]
    row_hot = (row_block.reshape(width)[None, :] == block_ids).astype(jnp.float32) * usable.reshape(
        width
    )[None, :]
    served_hot = (served_block.reshape(width)[None, :] == block_ids).astype(
        jnp.float32
    ) * served_ok.reshape(width)[None, :]
    groups = width // 32
    local_geo_groups = local_geo.reshape(groups, 32, 7, BLK)
    remote_geo_groups = remote_geo.reshape(groups, 32, 7, BLK)
    mask_groups = usable.reshape(groups, 32)
    radiosity = emission
    for sweep in range(ITERS):
        flux = (area[None, :] * radiosity).astype(jnp.bfloat16)
        flux_blocks = jnp.transpose(flux.reshape(BANDS, nblocks, BLK), (1, 0, 2))
        leaving = flux_blocks[row_block]
        arriving = move_flux(flux_blocks[served_block])

        def one_group(carry, item):
            row_geo, col_geo, col_flux, row_flux, mask_here = item
            tiles = jax.vmap(view_tile)(row_geo, col_geo) * mask_here[:, None, None]
            tiles = tiles.astype(jnp.bfloat16)
            own = jnp.einsum("sbj,sij->sbi", col_flux, tiles, preferred_element_type=jnp.float32)
            back = jnp.einsum("sbi,sij->sbj", row_flux, tiles, preferred_element_type=jnp.float32)
            return (carry, (own, back))

        items = (
            local_geo_groups,
            remote_geo_groups,
            arriving.reshape(groups, 32, BANDS, BLK),
            leaving.reshape(groups, 32, BANDS, BLK),
            mask_groups,
        )
        unused, terms = lax.scan(one_group, jnp.zeros((), jnp.float32), items)
        own_terms, back_terms = terms
        returned = move_back(back_terms.reshape(peers, CAP, BANDS, BLK))
        local_sum = jnp.dot(
            row_hot, own_terms.reshape(width, BANDS * BLK), precision=lax.Precision.HIGHEST
        )
        returned_sum = jnp.dot(
            served_hot, returned.reshape(width, BANDS * BLK), precision=lax.Precision.HIGHEST
        )
        summed = (local_sum + returned_sum).reshape(nblocks, BANDS, BLK)
        irradiation = jnp.transpose(summed, (1, 0, 2)).reshape(BANDS, patches)
        radiosity = emission + reflect * irradiation
    return radiosity


def solution(mesh):
    placed = (
        P(None, ("gx", "gy")),
        P(None, ("gx", "gy")),
        P(None, ("gx", "gy")),
        P(("gx", "gy")),
        P(("gx", "gy")),
        P(),
        P(),
        P(("gx", "gy"), None, None, None),
    )
    return jax.shard_map(
        per_device, mesh=mesh, in_specs=placed, out_specs=P(None, ("gx", "gy")), check_vma=False
    )
```

profile of v0, /device:TPU:1, one launch (start us, length us, event | category | flops | bytes accessed | tf_op | source)
XLA Modules:
  0.0 662.8 jit_solution(17341751652082272167)
XLA Ops:
  1.5 11.5 %all-to-all-start = ((s32[128,1,2]{2,1,0:T(1,128)}), s32[128,1,2]{2,1,0:T(1,128)S(1)}, u32[]{:S(2)}, u32[]{:S(2)}) async-start(s32[128,1,2]{2,1,0:T(1,128)} %bitcast.45), calls=%async_computation | async-start | bytes 131072 | tf_op jit(solution)/shard_map/all_to_all | solution.py:67
  14.6 7.9 %all-to-all-done = s32[128,1,2]{2,1,0:T(1,128)S(1)} async-done(((s32[128,1,2]{2,1,0:T(1,128)}), s32[128,1,2]{2,1,0:T(1,128)S(1)}, u32[]{:S(2)}, u32[]{:S(2)}) %all-to-all-start) | async-done | bytes 1056 | tf_op jit(solution)/shard_map/all_to_all | solution.py:67
  29.1 5.2 all-to-all-start.2
  36.4 25.4 %all-to-all-done.2 = f32[128,2,7,256]{3,1,2,0:T(2,128)} async-done(((f32[128,2,7,256]{3,1,2,0:T(2,128)}), f32[128,2,7,256]{3,1,2,0:T(2,128)}, u32[]{:S(2)}, u32[]{:S(2)}) %all-to-all-start.2) | async-done | bytes 1835040 | tf_op jit(solution)/shard_map/all_to_all | solution.py:72
  61.9 5.4 all-to-all-start.1
  86.4 11.2 %all-to-all-done.1 = bf16[128,2,16,256]{3,2,1,0:T(8,128)(2,1)} async-done(((bf16[128,2,16,256]{3,2,1,0:T(8,128)(2,1)}), bf16[128,2,16,256]{3,2,1,0:T(8,128)(2,1)}, u32[]{:S(2)}, u32[]{:S(2)}) %all-to-all-start.1) | async-done | bytes 2097184 | tf_op jit(solution)/shard_map/all_to_all | solution.py:36
  100.1 221.0 %while.24 = (s32[]{:T(128)}, f32[8,32,16,256]{3,2,1,0:T(8,128)}, bf16[8,32,16,256]{3,2,1,0:T(8,128)(2,1)}, bf16[8,32,16,256]{3,2,1,0:T(8,128)(2,1)}, f32[8,32,7,...) while((s32[]{:T(128)}, f32[8,32,16,256]{3,2,1,0:T(8,128)}, ...), condition=%wide.region_2.3_spmd, body=%wide.region_1.2_spmd.sunk | while | flops 264241152 | bytes 4328045 | solution.py:108
  101.1 13.3 %fusion.106 = bf16[8,32,16,256]{3,2,1,0:T(8,128)(2,1)} fusion(bf16[8,32,16,256]{3,2,1,0:T(8,128)(2,1)} %get-tuple-element.386, s32[]{:T(128)S(6)} %copy.68, bf16[8,32,16,256]{3,2,1,0:T(8,128)(2,1)} %get-tuple-element.400, f32[32]{0:T(128)S(1)} %fusion.104, f32[32,256]{1,0:T(8,128)S(1)} %get-tuple-element.336, f32[32,256]{1,0:T(8,128)S(1)} %get-tuple-element.338, ...), kind=kOutput, calls=%fused_computation.33.clone.1 | convolution fusion | flops 132120576 | bytes 1246336 | tf_op jit(solution)/shard_map/while/body/eval_jaxpr/sbi,sij->sbj/dot_general | solution.py:98
  114.4 13.3 %fusion.105 = f32[8,32,16,256]{3,2,1,0:T(8,128)} fusion(f32[8,32,16,256]{3,2,1,0:T(8,128)} %get-tuple-element.385, s32[]{:T(128)S(6)} %copy.68, bf16[8,32,16,256]{3,2,1,0:T(8,128)(2,1)} %get-tuple-element.396, f32[32]{0:T(128)S(1)} %fusion.104, f32[32,256]{1,0:T(8,128)S(1)} %get-tuple-element.336, f32[32,256]{1,0:T(8,128)S(1)} %get-tuple-element.338, ...), kind=kOutput, calls=%fused_computation.35.clone.1 | convolution fusion | flops 132120576 | bytes 1246336 | tf_op jit(solution)/shard_map/while/body/eval_jaxpr/sbj,sij->sbi/dot_general | solution.py:97
  128.8 13.3 %fusion.106 = bf16[8,32,16,256]{3,2,1,0:T(8,128)(2,1)} fusion(bf16[8,32,16,256]{3,2,1,0:T(8,128)(2,1)} %get-tuple-element.386, s32[]{:T(128)S(6)} %copy.68, bf16[8,32,16,256]{3,2,1,0:T(8,128)(2,1)} %get-tuple-element.400, f32[32]{0:T(128)S(1)} %fusion.104, f32[32,256]{1,0:T(8,128)S(1)} %get-tuple-element.336, f32[32,256]{1,0:T(8,128)S(1)} %get-tuple-element.338, ...), kind=kOutput, calls=%fused_computation.33.clone.1 | convolution fusion | flops 132120576 | bytes 1246336 | tf_op jit(solution)/shard_map/while/body/eval_jaxpr/sbi,sij->sbj/dot_general | solution.py:98
  142.0 13.3 %fusion.105 = f32[8,32,16,256]{3,2,1,0:T(8,128)} fusion(f32[8,32,16,256]{3,2,1,0:T(8,128)} %get-tuple-element.385, s32[]{:T(128)S(6)} %copy.68, bf16[8,32,16,256]{3,2,1,0:T(8,128)(2,1)} %get-tuple-element.396, f32[32]{0:T(128)S(1)} %fusion.104, f32[32,256]{1,0:T(8,128)S(1)} %get-tuple-element.336, f32[32,256]{1,0:T(8,128)S(1)} %get-tuple-element.338, ...), kind=kOutput, calls=%fused_computation.35.clone.1 | convolution fusion | flops 132120576 | bytes 1246336 | tf_op jit(solution)/shard_map/while/body/eval_jaxpr/sbj,sij->sbi/dot_general | solution.py:97
  156.4 13.3 %fusion.106 = bf16[8,32,16,256]{3,2,1,0:T(8,128)(2,1)} fusion(bf16[8,32,16,256]{3,2,1,0:T(8,128)(2,1)} %get-tuple-element.386, s32[]{:T(128)S(6)} %copy.68, bf16[8,32,16,256]{3,2,1,0:T(8,128)(2,1)} %get-tuple-element.400, f32[32]{0:T(128)S(1)} %fusion.104, f32[32,256]{1,0:T(8,128)S(1)} %get-tuple-element.336, f32[32,256]{1,0:T(8,128)S(1)} %get-tuple-element.338, ...), kind=kOutput, calls=%fused_computation.33.clone.1 | convolution fusion | flops 132120576 | bytes 1246336 | tf_op jit(solution)/shard_map/while/body/eval_jaxpr/sbi,sij->sbj/dot_general | solution.py:98
  169.7 13.3 %fusion.105 = f32[8,32,16,256]{3,2,1,0:T(8,128)} fusion(f32[8,32,16,256]{3,2,1,0:T(8,128)} %get-tuple-element.385, s32[]{:T(128)S(6)} %copy.68, bf16[8,32,16,256]{3,2,1,0:T(8,128)(2,1)} %get-tuple-element.396, f32[32]{0:T(128)S(1)} %fusion.104, f32[32,256]{1,0:T(8,128)S(1)} %get-tuple-element.336, f32[32,256]{1,0:T(8,128)S(1)} %get-tuple-element.338, ...), kind=kOutput, calls=%fused_computation.35.clone.1 | convolution fusion | flops 132120576 | bytes 1246336 | tf_op jit(solution)/shard_map/while/body/eval_jaxpr/sbj,sij->sbi/dot_general | solution.py:97
  184.0 13.3 %fusion.106 = bf16[8,32,16,256]{3,2,1,0:T(8,128)(2,1)} fusion(bf16[8,32,16,256]{3,2,1,0:T(8,128)(2,1)} %get-tuple-element.386, s32[]{:T(128)S(6)} %copy.68, bf16[8,32,16,256]{3,2,1,0:T(8,128)(2,1)} %get-tuple-element.400, f32[32]{0:T(128)S(1)} %fusion.104, f32[32,256]{1,0:T(8,128)S(1)} %get-tuple-element.336, f32[32,256]{1,0:T(8,128)S(1)} %get-tuple-element.338, ...), kind=kOutput, calls=%fused_computation.33.clone.1 | convolution fusion | flops 132120576 | bytes 1246336 | tf_op jit(solution)/shard_map/while/body/eval_jaxpr/sbi,sij->sbj/dot_general | solution.py:98
  197.3 13.3 %fusion.105 = f32[8,32,16,256]{3,2,1,0:T(8,128)} fusion(f32[8,32,16,256]{3,2,1,0:T(8,128)} %get-tuple-element.385, s32[]{:T(128)S(6)} %copy.68, bf16[8,32,16,256]{3,2,1,0:T(8,128)(2,1)} %get-tuple-element.396, f32[32]{0:T(128)S(1)} %fusion.104, f32[32,256]{1,0:T(8,128)S(1)} %get-tuple-element.336, f32[32,256]{1,0:T(8,128)S(1)} %get-tuple-element.338, ...), kind=kOutput, calls=%fused_computation.35.clone.1 | convolution fusion | flops 132120576 | bytes 1246336 | tf_op jit(solution)/shard_map/while/body/eval_jaxpr/sbj,sij->sbi/dot_general | solution.py:97
  211.6 13.3 %fusion.106 = bf16[8,32,16,256]{3,2,1,0:T(8,128)(2,1)} fusion(bf16[8,32,16,256]{3,2,1,0:T(8,128)(2,1)} %get-tuple-element.386, s32[]{:T(128)S(6)} %copy.68, bf16[8,32,16,256]{3,2,1,0:T(8,128)(2,1)} %get-tuple-element.400, f32[32]{0:T(128)S(1)} %fusion.104, f32[32,256]{1,0:T(8,128)S(1)} %get-tuple-element.336, f32[32,256]{1,0:T(8,128)S(1)} %get-tuple-element.338, ...), kind=kOutput, calls=%fused_computation.33.clone.1 | convolution fusion | flops 132120576 | bytes 1246336 | tf_op jit(solution)/shard_map/while/body/eval_jaxpr/sbi,sij->sbj/dot_general | solution.py:98
  224.9 13.3 %fusion.105 = f32[8,32,16,256]{3,2,1,0:T(8,128)} fusion(f32[8,32,16,256]{3,2,1,0:T(8,128)} %get-tuple-element.385, s32[]{:T(128)S(6)} %copy.68, bf16[8,32,16,256]{3,2,1,0:T(8,128)(2,1)} %get-tuple-element.396, f32[32]{0:T(128)S(1)} %fusion.104, f32[32,256]{1,0:T(8,128)S(1)} %get-tuple-element.336, f32[32,256]{1,0:T(8,128)S(1)} %get-tuple-element.338, ...), kind=kOutput, calls=%fused_computation.35.clone.1 | convolution fusion | flops 132120576 | bytes 1246336 | tf_op jit(solution)/shard_map/while/body/eval_jaxpr/sbj,sij->sbi/dot_general | solution.py:97
  239.2 13.3 %fusion.106 = bf16[8,32,16,256]{3,2,1,0:T(8,128)(2,1)} fusion(bf16[8,32,16,256]{3,2,1,0:T(8,128)(2,1)} %get-tuple-element.386, s32[]{:T(128)S(6)} %copy.68, bf16[8,32,16,256]{3,2,1,0:T(8,128)(2,1)} %get-tuple-element.400, f32[32]{0:T(128)S(1)} %fusion.104, f32[32,256]{1,0:T(8,128)S(1)} %get-tuple-element.336, f32[32,256]{1,0:T(8,128)S(1)} %get-tuple-element.338, ...), kind=kOutput, calls=%fused_computation.33.clone.1 | convolution fusion | flops 132120576 | bytes 1246336 | tf_op jit(solution)/shard_map/while/body/eval_jaxpr/sbi,sij->sbj/dot_general | solution.py:98
  252.5 13.3 %fusion.105 = f32[8,32,16,256]{3,2,1,0:T(8,128)} fusion(f32[8,32,16,256]{3,2,1,0:T(8,128)} %get-tuple-element.385, s32[]{:T(128)S(6)} %copy.68, bf16[8,32,16,256]{3,2,1,0:T(8,128)(2,1)} %get-tuple-element.396, f32[32]{0:T(128)S(1)} %fusion.104, f32[32,256]{1,0:T(8,128)S(1)} %get-tuple-element.336, f32[32,256]{1,0:T(8,128)S(1)} %get-tuple-element.338, ...), kind=kOutput, calls=%fused_computation.35.clone.1 | convolution fusion | flops 132120576 | bytes 1246336 | tf_op jit(solution)/shard_map/while/body/eval_jaxpr/sbj,sij->sbi/dot_general | solution.py:97
  266.8 13.3 %fusion.106 = bf16[8,32,16,256]{3,2,1,0:T(8,128)(2,1)} fusion(bf16[8,32,16,256]{3,2,1,0:T(8,128)(2,1)} %get-tuple-element.386, s32[]{:T(128)S(6)} %copy.68, bf16[8,32,16,256]{3,2,1,0:T(8,128)(2,1)} %get-tuple-element.400, f32[32]{0:T(128)S(1)} %fusion.104, f32[32,256]{1,0:T(8,128)S(1)} %get-tuple-element.336, f32[32,256]{1,0:T(8,128)S(1)} %get-tuple-element.338, ...), kind=kOutput, calls=%fused_computation.33.clone.1 | convolution fusion | flops 132120576 | bytes 1246336 | tf_op jit(solution)/shard_map/while/body/eval_jaxpr/sbi,sij->sbj/dot_general | solution.py:98
  280.1 13.3 %fusion.105 = f32[8,32,16,256]{3,2,1,0:T(8,128)} fusion(f32[8,32,16,256]{3,2,1,0:T(8,128)} %get-tuple-element.385, s32[]{:T(128)S(6)} %copy.68, bf16[8,32,16,256]{3,2,1,0:T(8,128)(2,1)} %get-tuple-element.396, f32[32]{0:T(128)S(1)} %fusion.104, f32[32,256]{1,0:T(8,128)S(1)} %get-tuple-element.336, f32[32,256]{1,0:T(8,128)S(1)} %get-tuple-element.338, ...), kind=kOutput, calls=%fused_computation.35.clone.1 | convolution fusion | flops 132120576 | bytes 1246336 | tf_op jit(solution)/shard_map/while/body/eval_jaxpr/sbj,sij->sbi/dot_general | solution.py:97
  294.5 13.3 %fusion.106 = bf16[8,32,16,256]{3,2,1,0:T(8,128)(2,1)} fusion(bf16[8,32,16,256]{3,2,1,0:T(8,128)(2,1)} %get-tuple-element.386, s32[]{:T(128)S(6)} %copy.68, bf16[8,32,16,256]{3,2,1,0:T(8,128)(2,1)} %get-tuple-element.400, f32[32]{0:T(128)S(1)} %fusion.104, f32[32,256]{1,0:T(8,128)S(1)} %get-tuple-element.336, f32[32,256]{1,0:T(8,128)S(1)} %get-tuple-element.338, ...), kind=kOutput, calls=%fused_computation.33.clone.1 | convolution fusion | flops 132120576 | bytes 1246336 | tf_op jit(solution)/shard_map/while/body/eval_jaxpr/sbi,sij->sbj/dot_general | solution.py:98
  307.8 13.3 %fusion.105 = f32[8,32,16,256]{3,2,1,0:T(8,128)} fusion(f32[8,32,16,256]{3,2,1,0:T(8,128)} %get-tuple-element.385, s32[]{:T(128)S(6)} %copy.68, bf16[8,32,16,256]{3,2,1,0:T(8,128)(2,1)} %get-tuple-element.396, f32[32]{0:T(128)S(1)} %fusion.104, f32[32,256]{1,0:T(8,128)S(1)} %get-tuple-element.336, f32[32,256]{1,0:T(8,128)S(1)} %get-tuple-element.338, ...), kind=kOutput, calls=%fused_computation.35.clone.1 | convolution fusion | flops 132120576 | bytes 1246336 | tf_op jit(solution)/shard_map/while/body/eval_jaxpr/sbj,sij->sbi/dot_general | solution.py:97
  321.1 5.6 all-to-all-start.3
  327.2 6.0 copy.51
  335.3 21.6 %all-to-all-done.3 = bf16[128,2,16,256]{3,2,1,0:T(8,128)(2,1)} async-done(((bf16[128,2,16,256]{3,2,1,0:T(8,128)(2,1)}), bf16[128,2,16,256]{3,2,1,0:T(8,128)(2,1)}, u32[]{:S(2)}, u32[]{:S(2)}) %all-to-all-start.3) | async-done | bytes 2097184 | tf_op jit(solution)/shard_map/all_to_all | solution.py:40
  363.6 5.4 all-to-all-start.4
  371.2 28.2 %all-to-all-done.4 = bf16[128,2,16,256]{3,2,1,0:T(8,128)(2,1)} async-done(((bf16[128,2,16,256]{3,2,1,0:T(8,128)(2,1)}), bf16[128,2,16,256]{3,2,1,0:T(8,128)(2,1)}, u32[]{:S(2)}, u32[]{:S(2)}) %all-to-all-start.4) | async-done | bytes 2097184 | tf_op jit(solution)/shard_map/all_to_all | solution.py:36
  401.8 221.0 %while.25 = (s32[]{:T(128)}, f32[8,32,16,256]{3,2,1,0:T(8,128)}, bf16[8,32,16,256]{3,2,1,0:T(8,128)(2,1)}, bf16[8,32,16,256]{3,2,1,0:T(8,128)(2,1)}, f32[8,32,7,...) while((s32[]{:T(128)}, f32[8,32,16,256]{3,2,1,0:T(8,128)}, ...), condition=%wide.region_4.5_spmd, body=%wide.region_3.4_spmd.sunk | while | flops 264241152 | bytes 4328045 | solution.py:108
  402.9 13.3 %fusion.113 = bf16[8,32,16,256]{3,2,1,0:T(8,128)(2,1)} fusion(bf16[8,32,16,256]{3,2,1,0:T(8,128)(2,1)} %get-tuple-element.413, s32[]{:T(128)S(6)} %copy.77, bf16[8,32,16,256]{3,2,1,0:T(8,128)(2,1)} %get-tuple-element.427, f32[32]{0:T(128)S(1)} %fusion.111, f32[32,256]{1,0:T(8,128)S(1)} %get-tuple-element.360, f32[32,256]{1,0:T(8,128)S(1)} %get-tuple-element.362, ...), kind=kOutput, calls=%fused_computation.87.clone.1 | convolution fusion | flops 132120576 | bytes 1246336 | tf_op jit(solution)/shard_map/while/body/eval_jaxpr/sbi,sij->sbj/dot_general | solution.py:98
  416.2 13.3 %fusion.112 = f32[8,32,16,256]{3,2,1,0:T(8,128)} fusion(f32[8,32,16,256]{3,2,1,0:T(8,128)} %get-tuple-element.412, s32[]{:T(128)S(6)} %copy.77, bf16[8,32,16,256]{3,2,1,0:T(8,128)(2,1)} %get-tuple-element.423, f32[32]{0:T(128)S(1)} %fusion.111, f32[32,256]{1,0:T(8,128)S(1)} %get-tuple-element.360, f32[32,256]{1,0:T(8,128)S(1)} %get-tuple-element.362, ...), kind=kOutput, calls=%fused_computation.89.clone.1 | convolution fusion | flops 132120576 | bytes 1246336 | tf_op jit(solution)/shard_map/while/body/eval_jaxpr/sbj,sij->sbi/dot_general | solution.py:97
  430.5 13.3 %fusion.113 = bf16[8,32,16,256]{3,2,1,0:T(8,128)(2,1)} fusion(bf16[8,32,16,256]{3,2,1,0:T(8,128)(2,1)} %get-tuple-element.413, s32[]{:T(128)S(6)} %copy.77, bf16[8,32,16,256]{3,2,1,0:T(8,128)(2,1)} %get-tuple-element.427, f32[32]{0:T(128)S(1)} %fusion.111, f32[32,256]{1,0:T(8,128)S(1)} %get-tuple-element.360, f32[32,256]{1,0:T(8,128)S(1)} %get-tuple-element.362, ...), kind=kOutput, calls=%fused_computation.87.clone.1 | convolution fusion | flops 132120576 | bytes 1246336 | tf_op jit(solution)/shard_map/while/body/eval_jaxpr/sbi,sij->sbj/dot_general | solution.py:98
  443.8 13.3 %fusion.112 = f32[8,32,16,256]{3,2,1,0:T(8,128)} fusion(f32[8,32,16,256]{3,2,1,0:T(8,128)} %get-tuple-element.412, s32[]{:T(128)S(6)} %copy.77, bf16[8,32,16,256]{3,2,1,0:T(8,128)(2,1)} %get-tuple-element.423, f32[32]{0:T(128)S(1)} %fusion.111, f32[32,256]{1,0:T(8,128)S(1)} %get-tuple-element.360, f32[32,256]{1,0:T(8,128)S(1)} %get-tuple-element.362, ...), kind=kOutput, calls=%fused_computation.89.clone.1 | convolution fusion | flops 132120576 | bytes 1246336 | tf_op jit(solution)/shard_map/while/body/eval_jaxpr/sbj,sij->sbi/dot_general | solution.py:97
  458.1 13.3 %fusion.113 = bf16[8,32,16,256]{3,2,1,0:T(8,128)(2,1)} fusion(bf16[8,32,16,256]{3,2,1,0:T(8,128)(2,1)} %get-tuple-element.413, s32[]{:T(128)S(6)} %copy.77, bf16[8,32,16,256]{3,2,1,0:T(8,128)(2,1)} %get-tuple-element.427, f32[32]{0:T(128)S(1)} %fusion.111, f32[32,256]{1,0:T(8,128)S(1)} %get-tuple-element.360, f32[32,256]{1,0:T(8,128)S(1)} %get-tuple-element.362, ...), kind=kOutput, calls=%fused_computation.87.clone.1 | convolution fusion | flops 132120576 | bytes 1246336 | tf_op jit(solution)/shard_map/while/body/eval_jaxpr/sbi,sij->sbj/dot_general | solution.py:98
  471.4 13.3 %fusion.112 = f32[8,32,16,256]{3,2,1,0:T(8,128)} fusion(f32[8,32,16,256]{3,2,1,0:T(8,128)} %get-tuple-element.412, s32[]{:T(128)S(6)} %copy.77, bf16[8,32,16,256]{3,2,1,0:T(8,128)(2,1)} %get-tuple-element.423, f32[32]{0:T(128)S(1)} %fusion.111, f32[32,256]{1,0:T(8,128)S(1)} %get-tuple-element.360, f32[32,256]{1,0:T(8,128)S(1)} %get-tuple-element.362, ...), kind=kOutput, calls=%fused_computation.89.clone.1 | convolution fusion | flops 132120576 | bytes 1246336 | tf_op jit(solution)/shard_map/while/body/eval_jaxpr/sbj,sij->sbi/dot_general | solution.py:97
  485.7 13.3 %fusion.113 = bf16[8,32,16,256]{3,2,1,0:T(8,128)(2,1)} fusion(bf16[8,32,16,256]{3,2,1,0:T(8,128)(2,1)} %get-tuple-element.413, s32[]{:T(128)S(6)} %copy.77, bf16[8,32,16,256]{3,2,1,0:T(8,128)(2,1)} %get-tuple-element.427, f32[32]{0:T(128)S(1)} %fusion.111, f32[32,256]{1,0:T(8,128)S(1)} %get-tuple-element.360, f32[32,256]{1,0:T(8,128)S(1)} %get-tuple-element.362, ...), kind=kOutput, calls=%fused_computation.87.clone.1 | convolution fusion | flops 132120576 | bytes 1246336 | tf_op jit(solution)/shard_map/while/body/eval_jaxpr/sbi,sij->sbj/dot_general | solution.py:98
  499.0 13.3 %fusion.112 = f32[8,32,16,256]{3,2,1,0:T(8,128)} fusion(f32[8,32,16,256]{3,2,1,0:T(8,128)} %get-tuple-element.412, s32[]{:T(128)S(6)} %copy.77, bf16[8,32,16,256]{3,2,1,0:T(8,128)(2,1)} %get-tuple-element.423, f32[32]{0:T(128)S(1)} %fusion.111, f32[32,256]{1,0:T(8,128)S(1)} %get-tuple-element.360, f32[32,256]{1,0:T(8,128)S(1)} %get-tuple-element.362, ...), kind=kOutput, calls=%fused_computation.89.clone.1 | convolution fusion | flops 132120576 | bytes 1246336 | tf_op jit(solution)/shard_map/while/body/eval_jaxpr/sbj,sij->sbi/dot_general | solution.py:97
  513.4 13.3 %fusion.113 = bf16[8,32,16,256]{3,2,1,0:T(8,128)(2,1)} fusion(bf16[8,32,16,256]{3,2,1,0:T(8,128)(2,1)} %get-tuple-element.413, s32[]{:T(128)S(6)} %copy.77, bf16[8,32,16,256]{3,2,1,0:T(8,128)(2,1)} %get-tuple-element.427, f32[32]{0:T(128)S(1)} %fusion.111, f32[32,256]{1,0:T(8,128)S(1)} %get-tuple-element.360, f32[32,256]{1,0:T(8,128)S(1)} %get-tuple-element.362, ...), kind=kOutput, calls=%fused_computation.87.clone.1 | convolution fusion | flops 132120576 | bytes 1246336 | tf_op jit(solution)/shard_map/while/body/eval_jaxpr/sbi,sij->sbj/dot_general | solution.py:98
  526.7 13.3 %fusion.112 = f32[8,32,16,256]{3,2,1,0:T(8,128)} fusion(f32[8,32,16,256]{3,2,1,0:T(8,128)} %get-tuple-element.412, s32[]{:T(128)S(6)} %copy.77, bf16[8,32,16,256]{3,2,1,0:T(8,128)(2,1)} %get-tuple-element.423, f32[32]{0:T(128)S(1)} %fusion.111, f32[32,256]{1,0:T(8,128)S(1)} %get-tuple-element.360, f32[32,256]{1,0:T(8,128)S(1)} %get-tuple-element.362, ...), kind=kOutput, calls=%fused_computation.89.clone.1 | convolution fusion | flops 132120576 | bytes 1246336 | tf_op jit(solution)/shard_map/while/body/eval_jaxpr/sbj,sij->sbi/dot_general | solution.py:97
  541.0 13.3 %fusion.113 = bf16[8,32,16,256]{3,2,1,0:T(8,128)(2,1)} fusion(bf16[8,32,16,256]{3,2,1,0:T(8,128)(2,1)} %get-tuple-element.413, s32[]{:T(128)S(6)} %copy.77, bf16[8,32,16,256]{3,2,1,0:T(8,128)(2,1)} %get-tuple-element.427, f32[32]{0:T(128)S(1)} %fusion.111, f32[32,256]{1,0:T(8,128)S(1)} %get-tuple-element.360, f32[32,256]{1,0:T(8,128)S(1)} %get-tuple-element.362, ...), kind=kOutput, calls=%fused_computation.87.clone.1 | convolution fusion | flops 132120576 | bytes 1246336 | tf_op jit(solution)/shard_map/while/body/eval_jaxpr/sbi,sij->sbj/dot_general | solution.py:98
  554.3 13.3 %fusion.112 = f32[8,32,16,256]{3,2,1,0:T(8,128)} fusion(f32[8,32,16,256]{3,2,1,0:T(8,128)} %get-tuple-element.412, s32[]{:T(128)S(6)} %copy.77, bf16[8,32,16,256]{3,2,1,0:T(8,128)(2,1)} %get-tuple-element.423, f32[32]{0:T(128)S(1)} %fusion.111, f32[32,256]{1,0:T(8,128)S(1)} %get-tuple-element.360, f32[32,256]{1,0:T(8,128)S(1)} %get-tuple-element.362, ...), kind=kOutput, calls=%fused_computation.89.clone.1 | convolution fusion | flops 132120576 | bytes 1246336 | tf_op jit(solution)/shard_map/while/body/eval_jaxpr/sbj,sij->sbi/dot_general | solution.py:97
  568.6 13.3 %fusion.113 = bf16[8,32,16,256]{3,2,1,0:T(8,128)(2,1)} fusion(bf16[8,32,16,256]{3,2,1,0:T(8,128)(2,1)} %get-tuple-element.413, s32[]{:T(128)S(6)} %copy.77, bf16[8,32,16,256]{3,2,1,0:T(8,128)(2,1)} %get-tuple-element.427, f32[32]{0:T(128)S(1)} %fusion.111, f32[32,256]{1,0:T(8,128)S(1)} %get-tuple-element.360, f32[32,256]{1,0:T(8,128)S(1)} %get-tuple-element.362, ...), kind=kOutput, calls=%fused_computation.87.clone.1 | convolution fusion | flops 132120576 | bytes 1246336 | tf_op jit(solution)/shard_map/while/body/eval_jaxpr/sbi,sij->sbj/dot_general | solution.py:98
  581.9 13.3 %fusion.112 = f32[8,32,16,256]{3,2,1,0:T(8,128)} fusion(f32[8,32,16,256]{3,2,1,0:T(8,128)} %get-tuple-element.412, s32[]{:T(128)S(6)} %copy.77, bf16[8,32,16,256]{3,2,1,0:T(8,128)(2,1)} %get-tuple-element.423, f32[32]{0:T(128)S(1)} %fusion.111, f32[32,256]{1,0:T(8,128)S(1)} %get-tuple-element.360, f32[32,256]{1,0:T(8,128)S(1)} %get-tuple-element.362, ...), kind=kOutput, calls=%fused_computation.89.clone.1 | convolution fusion | flops 132120576 | bytes 1246336 | tf_op jit(solution)/shard_map/while/body/eval_jaxpr/sbj,sij->sbi/dot_general | solution.py:97
  596.2 13.3 %fusion.113 = bf16[8,32,16,256]{3,2,1,0:T(8,128)(2,1)} fusion(bf16[8,32,16,256]{3,2,1,0:T(8,128)(2,1)} %get-tuple-element.413, s32[]{:T(128)S(6)} %copy.77, bf16[8,32,16,256]{3,2,1,0:T(8,128)(2,1)} %get-tuple-element.427, f32[32]{0:T(128)S(1)} %fusion.111, f32[32,256]{1,0:T(8,128)S(1)} %get-tuple-element.360, f32[32,256]{1,0:T(8,128)S(1)} %get-tuple-element.362, ...), kind=kOutput, calls=%fused_computation.87.clone.1 | convolution fusion | flops 132120576 | bytes 1246336 | tf_op jit(solution)/shard_map/while/body/eval_jaxpr/sbi,sij->sbj/dot_general | solution.py:98
  609.5 13.3 %fusion.112 = f32[8,32,16,256]{3,2,1,0:T(8,128)} fusion(f32[8,32,16,256]{3,2,1,0:T(8,128)} %get-tuple-element.412, s32[]{:T(128)S(6)} %copy.77, bf16[8,32,16,256]{3,2,1,0:T(8,128)(2,1)} %get-tuple-element.423, f32[32]{0:T(128)S(1)} %fusion.111, f32[32,256]{1,0:T(8,128)S(1)} %get-tuple-element.360, f32[32,256]{1,0:T(8,128)S(1)} %get-tuple-element.362, ...), kind=kOutput, calls=%fused_computation.89.clone.1 | convolution fusion | flops 132120576 | bytes 1246336 | tf_op jit(solution)/shard_map/while/body/eval_jaxpr/sbj,sij->sbi/dot_general | solution.py:97
  622.8 5.4 all-to-all-start.5
  628.3 6.0 copy.54
  636.4 22.2 %all-to-all-done.5 = bf16[128,2,16,256]{3,2,1,0:T(8,128)(2,1)} async-done(((bf16[128,2,16,256]{3,2,1,0:T(8,128)(2,1)}), bf16[128,2,16,256]{3,2,1,0:T(8,128)(2,1)}, u32[]{:S(2)}, u32[]{:S(2)}) %all-to-all-start.5) | async-done | bytes 2097184 | tf_op jit(solution)/shard_map/all_to_all | solution.py:40
  (158 shorter events, 69.9 us)
Async XLA Ops:
  0.0 360.5 %copy-start = (f32[8,16]{1,0:T(8,128)S(1)}, f32[8,16]{1,0:T(8,128)}, u32[]{:S(2)}) copy-start(f32[8,16]{1,0:T(8,128)} %param.17) | copy-start | bytes 1540
  1.5 21.0 %all-to-all-start = ((s32[128,1,2]{2,1,0:T(1,128)}), s32[128,1,2]{2,1,0:T(1,128)S(1)}, u32[]{:S(2)}, u32[]{:S(2)}) async-start(s32[128,1,2]{2,1,0:T(1,128)} %bitcast.45), calls=%async_computation | async-start | bytes 131072 | tf_op jit(solution)/shard_map/all_to_all | solution.py:67
  13.8 20.5 %copy-start.13 = (f32[2048]{0:T(1024)}, f32[2048]{0:T(1024)S(1)}, u32[]{:S(2)}) copy-start(f32[2048]{0:T(1024)S(1)} %select_reduce_fusion) | copy-start | bytes 24580
  22.5 6.5 copy-start.8
  22.9 6.2 copy-start.15
  22.9 11.4 %copy-start.1 = (s32[1024]{0:T(1024)}, s32[1024]{0:T(1024)S(1)}, u32[]{:S(2)}) copy-start(s32[1024]{0:T(1024)S(1)} %pad_clamp_fusion.1) | copy-start | bytes 12292
  25.3 9.0 %copy-start.5 = (f32[16,2048]{1,0:T(8,128)S(1)}, f32[16,2048]{1,0:T(8,128)}, u32[]{:S(2)}) copy-start(f32[16,2048]{1,0:T(8,128)} %param.14) | copy-start | bytes 393220
  29.1 32.8 %all-to-all-start.2 = ((f32[128,2,7,256]{3,1,2,0:T(2,128)}), f32[128,2,7,256]{3,1,2,0:T(2,128)}, u32[]{:S(2)}, u32[]{:S(2)}) async-start(f32[128,2,7,256]{3,1,2,0:T(2,128)} %copy.40), calls=%async_computation.2 | async-start | bytes 3670016 | tf_op jit(solution)/shard_map/all_to_all | solution.py:72
  61.9 35.7 %all-to-all-start.1 = ((bf16[128,2,16,256]{3,2,1,0:T(8,128)(2,1)}), bf16[128,2,16,256]{3,2,1,0:T(8,128)(2,1)}, u32[]{:S(2)}, u32[]{:S(2)}) async-start(bf16[128,2,16,256]{3,2,1,0:T(8,128)(2,1)} %bitcast.206), calls=%async_computation.1 | async-start | bytes 4194304 | tf_op jit(solution)/shard_map/all_to_all | solution.py:36
  67.4 4.5 copy-start.18
  67.4 4.5 copy-start.3
  71.9 4.8 copy-start.10
  321.0 5.6 copy-start.11
  321.0 5.8 copy-start.9
  321.1 35.9 %all-to-all-start.3 = ((bf16[128,2,16,256]{3,2,1,0:T(8,128)(2,1)}), bf16[128,2,16,256]{3,2,1,0:T(8,128)(2,1)}, u32[]{:S(2)}, u32[]{:S(2)}) async-start(bf16[128,2,16,256]{3,2,1,0:T(8,128)(2,1)} %bitcast.207), calls=%async_computation.3 | async-start | bytes 4194304 | tf_op jit(solution)/shard_map/all_to_all | solution.py:40
  326.8 6.4 copy-start.23
  327.2 32.3 %copy-start.21 = (f32[256]{0:T(256)}, f32[256]{0:T(256)S(1)}, u32[]{:S(2)}) copy-start(f32[256]{0:T(256)S(1)} %reshape.152) | copy-start | bytes 3076
  327.2 6.0 copy-start.19
  333.2 26.3 %copy-start.16 = (s32[256]{0:T(256)S(1)}, s32[256]{0:T(256)}, u32[]{:S(2)}) copy-start(s32[256]{0:T(256)} %copy-done.15) | copy-start | bytes 3076
  335.3 25.2 %copy-start.6 = (f32[16,2048]{1,0:T(8,128)S(1)}, f32[16,2048]{1,0:T(8,128)}, u32[]{:S(2)}) copy-start(f32[16,2048]{1,0:T(8,128)} %param.14) | copy-start | bytes 393220
  335.3 25.2 %copy-start.14 = (f32[2048]{0:T(1024)S(1)}, f32[2048]{0:T(1024)}, u32[]{:S(2)}) copy-start(f32[2048]{0:T(1024)} %copy-done.13) | copy-start | bytes 24580
  335.3 25.2 %copy-start.25 = (s32[2048]{0:T(1024)S(1)}, s32[2048]{0:T(1024)}, u32[]{:S(2)}) copy-start(s32[2048]{0:T(1024)} %param.15) | copy-start | bytes 24580
  335.3 26.1 %copy-start.2 = (s32[1024]{0:T(1024)S(1)}, s32[1024]{0:T(1024)}, u32[]{:S(2)}) copy-start(s32[1024]{0:T(1024)} %copy-done.1) | copy-start | bytes 12292
  361.4 7.6 %copy-start.4 = (s32[1024]{0:T(1024)S(1)}, s32[1024]{0:T(1024)}, u32[]{:S(2)}) copy-start(s32[1024]{0:T(1024)} %copy-done.3) | copy-start | bytes 12292
  363.6 35.7 %all-to-all-start.4 = ((bf16[128,2,16,256]{3,2,1,0:T(8,128)(2,1)}), bf16[128,2,16,256]{3,2,1,0:T(8,128)(2,1)}, u32[]{:S(2)}, u32[]{:S(2)}) async-start(bf16[128,2,16,256]{3,2,1,0:T(8,128)(2,1)} %bitcast.209), calls=%async_computation.4 | async-start | bytes 4194304 | tf_op jit(solution)/shard_map/all_to_all | solution.py:36
  622.8 35.7 %all-to-all-start.5 = ((bf16[128,2,16,256]{3,2,1,0:T(8,128)(2,1)}), bf16[128,2,16,256]{3,2,1,0:T(8,128)(2,1)}, u32[]{:S(2)}, u32[]{:S(2)}) async-start(bf16[128,2,16,256]{3,2,1,0:T(8,128)(2,1)} %bitcast.64), calls=%async_computation.5 | async-start | bytes 4194304 | tf_op jit(solution)/shard_map/all_to_all | solution.py:40
  628.3 6.0 copy-start.20
  628.3 6.0 copy-start.24
  634.3 26.8 %copy-start.17 = (s32[256]{0:T(256)S(1)}, s32[256]{0:T(256)}, u32[]{:S(2)}) copy-start(s32[256]{0:T(256)} %copy-done.15) | copy-start | bytes 3076
  634.3 26.8 %copy-start.22 = (f32[256]{0:T(256)S(1)}, f32[256]{0:T(256)}, u32[]{:S(2)}) copy-start(f32[256]{0:T(256)} %copy-done.21) | copy-start | bytes 3076
  636.4 25.7 %copy-start.7 = (f32[16,2048]{1,0:T(8,128)S(1)}, f32[16,2048]{1,0:T(8,128)}, u32[]{:S(2)}) copy-start(f32[16,2048]{1,0:T(8,128)} %param.14) | copy-start | bytes 393220
  636.4 25.7 %copy-start.12 = (f32[16,2048]{1,0:T(8,128)S(1)}, f32[16,2048]{1,0:T(8,128)}, u32[]{:S(2)}) copy-start(f32[16,2048]{1,0:T(8,128)} %get-tuple-element.212) | copy-start | bytes 393220
where the time goes:
time: 666 us; the launch traced here: 663 us
  matrix products  432 us (65%)
  waiting for transfers between devices  117 us (18%)
  local copies, waits for them, and re-layouts  70 us (11%)
  starting transfers between devices  38.5 us (6%)
    dot_general x16, matrix products, one_group(): jnp.einsum('sbi,sij->sbj', row_flux, tiles, preferred_element_type=jnp.fl...  213 us
    dot_general x16, matrix products, one_group(): jnp.einsum('sbj,sij->sbi', col_flux, tiles, preferred_element_type=jnp.fl...  212 us
    all_to_all x2, waiting for transfers between devices, move_back(): lax.all_to_all(blocks.astype(jnp.bfloat16), ('gx', 'gy'), split_axis=0, c...  43.8 us
    all_to_all x2, waiting for transfers between devices, move_flux(): lax.all_to_all(blocks, ('gx', 'gy'), split_axis=0, concat_axis=0, tiled=T...  39.4 us
    all_to_all x1, waiting for transfers between devices, per_device(): lax.all_to_all(requested_geo, ('gx', 'gy'), split_axis=0, concat_axis=0,...  25.4 us
    unnamed x60, local copies, waits for them, and re-layouts  21.1 us
    squeeze x16, local copies, waits for them, and re-layouts, per_device(): unused, terms = lax.scan(one_group, jnp.zeros((), jnp.float32), items)  15.9 us
  transfers between devices with their start and end apart: 6, of which 6 were waited for; matrix products, arithmetic and copies ran while one was open for 6% of the time, Pallas kernels for 0%

commit v1 on v0

v1 whole, which is shorter than its diff:
```python
import functools
import math

import jax
import jax.numpy as jnp
from jax import lax
from jax.experimental import pallas as pl
from jax.experimental.pallas import tpu as pltpu
from jax.sharding import PartitionSpec as P

MESH = pl.DeviceIdType.MESH
BANDS = 16
BLK = 256
HALF = 128
ITERS = 2
AXES = ("gx", "gy")
SIDE = 4
ORDERS = (("x", "y", "z"), ("y", "z", "x"), ("z", "x", "y"))
FLUX_PARTS = (6, 5, 5)
GEO_PARTS = (5, 6, 5)
KEPT = 336
STEP = 4
STEP2 = 8
CHUNK = 64
KAPPA = (math.pi - 1.0) / math.pi


def my_place():
    z = lax.axis_index("gx")
    inner = lax.axis_index("gy")
    place = {"z": z, "y": lax.div(inner, 2 * SIDE), "x": lax.rem(lax.div(inner, 2), SIDE)}
    return place, lax.rem(inner, 2)


def device_of(place, core):
    return (place["z"], (place["y"] * SIDE + place["x"]) * 2 + core)


def moved(place, axis, by):
    other = dict(place)
    other[axis] = lax.rem(place[axis] + (by + SIDE), SIDE)
    return other


def gather_kernel(parts, count, *refs):
    srcs, bufs = refs[:count], refs[count : 2 * count]
    send_sem, recv_sem, local_sem = refs[2 * count :]
    here, core = my_place()
    other_core = device_of(here, 1 - core)
    own_copies = []
    for b in range(count):
        place = bufs[b].at[here["z"], here["y"], here["x"], core]
        own_copies.append(pltpu.make_async_copy(srcs[b], place, local_sem.at[b]))
        own_copies[-1].start()
    barrier = pltpu.get_barrier_semaphore()
    peers = [device_of(moved(here, axis, by), core) for axis in "zyx" for by in (1, -1)]
    peers.append(other_core)
    for peer in peers:
        pl.semaphore_signal(barrier, inc=1, device_id=peer, device_id_type=MESH)
    pl.semaphore_wait(barrier, len(peers))
    started = []
    shared = []

    def send(src, dst, to):
        n = len(started)
        copy = pltpu.make_async_remote_copy(
            src_ref=src,
            dst_ref=dst,
            send_sem=send_sem.at[n],
            recv_sem=recv_sem.at[n],
            device_id=to,
            device_id_type=MESH,
        )
        copy.start()
        started.append(copy)
        return copy

    def view(b, index, first, size):
        return bufs[b].at[index["z"], index["y"], index["x"], core, pl.ds(first, size)]

    def share(b, index, first, size):
        piece = view(b, index, first, size)
        shared.append(send(piece, piece, other_core))

    work = []
    for b in range(count):
        first = 0
        for k, size in enumerate(parts[b]):
            work.append((b, k, first, size))
            first += size

    def group(phase, k, by):
        order = ORDERS[k]
        index = moved(here, order[phase], by)
        for axis in order[:phase]:
            index[axis] = pl.ds(0, SIDE)
        return index

    def half_of(phase, k, index, first, size, which):
        if phase == 0:
            low = (size + 1) // 2
            return (index, first, low) if which == 0 else (index, first + low, size - low)
        index = dict(index)
        index[ORDERS[k][0]] = pl.ds(2 * which, 2)
        return index, first, size

    for phase in range(3):
        up, down, up2, down2 = {}, {}, {}, {}
        for item in work:
            b, k, first, size = item
            axis = ORDERS[k][phase]
            dst = view(b, group(phase, k, 0), first, size)
            src = dst if phase else srcs[b].at[pl.ds(first, size)]
            up[item] = send(src, dst, device_of(moved(here, axis, 1), core))
            down[item] = send(src, dst, device_of(moved(here, axis, -1), core))
        if phase == 0:
            for b in range(count):
                place = bufs[b].at[here["z"], here["y"], here["x"], core]
                shared.append(send(srcs[b], place, other_core))
            for copy in own_copies:
                copy.wait()
        for item in work:
            b, k, first, size = item
            axis = ORDERS[k][phase]
            below, above = group(phase, k, -1), group(phase, k, 1)
            up[item].wait_recv()
            piece = view(b, *half_of(phase, k, below, first, size, 0))
            up2[item] = send(piece, piece, device_of(moved(here, axis, 1), core))
            down[item].wait_recv()
            piece = view(b, *half_of(phase, k, above, first, size, 1))
            down2[item] = send(piece, piece, device_of(moved(here, axis, -1), core))
            share(b, below, first, size)
            share(b, above, first, size)
        for item in work:
            b, k, first, size = item
            up2[item].wait_recv()
            down2[item].wait_recv()
            share(b, group(phase, k, 2), first, size)
    for copy in shared:
        copy.wait_recv()
    for copy in started:
        copy.wait_send()


def gather_all(arrays, parts, collective_id):
    count = len(arrays)
    copies = (3 * 7 * 3 + 1) * count
    anywhere = pl.BlockSpec(memory_space=pl.ANY)
    return pl.pallas_call(
        functools.partial(gather_kernel, parts, count),
        out_shape=[
            jax.ShapeDtypeStruct((SIDE, SIDE, SIDE, 2) + a.shape, a.dtype) for a in arrays
        ],
        in_specs=[anywhere] * count,
        out_specs=[anywhere] * count,
        scratch_shapes=[
            pltpu.SemaphoreType.DMA((copies,)),
            pltpu.SemaphoreType.DMA((copies,)),
            pltpu.SemaphoreType.DMA((count,)),
        ],
        compiler_params=pltpu.CompilerParams(collective_id=collective_id, has_side_effects=True),
        name="gather_all",
    )(*arrays)


def split3(x):
    a = x.astype(jnp.bfloat16).astype(jnp.float32)
    rest = x - a
    b = rest.astype(jnp.bfloat16).astype(jnp.float32)
    return a, b, rest - b


def block_of(ref, b):
    return jnp.concatenate([ref[b, 0], ref[b, 1]], axis=1)


def centred(rows, centre):
    moved_rows = rows - centre
    squares = moved_rows * moved_rows
    cross = moved_rows * pltpu.roll(moved_rows, 4, 0)
    reach = (squares[0:1] + squares[1:2] + squares[2:3]) + 0.5 * rows[3:4]
    plane = -(cross[0:1] + cross[1:2] + cross[2:3])
    return moved_rows, reach, plane


def source_rows(rows, centre):
    at = lax.broadcasted_iota(jnp.int32, rows.shape, 0)
    base, reach, plane = centred(rows, centre)
    base = jnp.where(at == 3, reach, jnp.where(at == 7, plane, base))
    a, b, c = split3(base)
    one = jnp.where(at < 3, 1.0, 0.0)
    stacked = jnp.concatenate([a, a, a, b, b, c, one, jnp.zeros_like(one)], axis=0)
    return stacked.astype(jnp.bfloat16), (KAPPA * 0.5) * rows[3:4]


def target_columns(rows, centre):
    at = lax.broadcasted_iota(jnp.int32, rows.shape, 0)
    base, reach, plane = centred(rows, centre)
    zero = jnp.zeros_like(base)
    swapped = pltpu.roll(base, 4, 0)
    facing = jnp.where(at < 3, swapped, 0.0) * (1.0 / math.pi)
    seen = jnp.where((at >= 4) & (at < 7), swapped, jnp.where(at == 7, 1.0, 0.0))
    spread = jnp.where(at < 3, -2.0 * base, jnp.where(at == 3, 1.0, 0.0))
    columns = []
    for factor, constant in ((facing, plane * (1.0 / math.pi)), (seen, None), (spread, reach)):
        a, b, c = split3(factor)
        last = zero
        if constant is not None:
            d, e, f = split3(constant)
            last = jnp.where(at == 0, d, jnp.where(at == 1, e, jnp.where(at == 2, f, 0.0)))
        stacked = jnp.concatenate([a, b, c, a, b, a, last, zero], axis=0)
        columns.append(jnp.transpose(stacked).astype(jnp.bfloat16))
    return columns, (KAPPA * 0.5) * rows[3:4]


def prepare_targets(own_ref, centre_ref, column_ref, offset_ref):
    for t in range(8):
        rows = block_of(own_ref, t)
        at = lax.broadcasted_iota(jnp.int32, rows.shape, 0)
        centre = jnp.where(at < 3, jnp.broadcast_to(rows[:, 0:1], rows.shape), 0.0)
        centre_ref[t] = centre
        columns, offset = target_columns(rows, centre)
        for r in range(0, BLK, CHUNK):
            column_ref[t, 3 * r : 3 * (r + CHUNK)] = jnp.concatenate(
                [c[r : r + CHUNK] for c in columns], axis=0
            )
        offset_ref[t] = jnp.transpose(jnp.broadcast_to(offset, (HALF, BLK)))


def build_tile(t, b, geo_ref, centre_ref, column_ref, offset_ref, tile_ref, slot):
    source, source_offset = source_rows(block_of(geo_ref, b), centre_ref[t])
    for r in range(0, BLK, CHUNK):
        terms = jnp.dot(
            column_ref[t, 3 * r : 3 * (r + CHUNK), :], source, preferred_element_type=jnp.float32
        )
        facing, seen, spread = terms[:CHUNK], terms[CHUNK : 2 * CHUNK], terms[2 * CHUNK :]
        offset = offset_ref[t, r : r + CHUNK, :]
        offset = jnp.concatenate([offset, offset], axis=1)
        over = jnp.maximum(facing, 0.0) * jnp.maximum(seen, 0.0)
        under = spread * ((spread - offset) - source_offset)
        inverse = pl.reciprocal(under, approx=True)
        inverse = inverse * (2.0 - under * inverse)
        tile_ref[slot, r : r + CHUNK, :] = (over * inverse).astype(jnp.bfloat16)


def add_product(t, flux, tile, sum_ref):
    term = lax.dot_general(
        flux, tile, (((1,), (1,)), ((), ())), preferred_element_type=jnp.float32
    )
    sum_ref[t, 0] += term[:, :HALF]
    sum_ref[t, 1] += term[:, HALF:]


def decode(code):
    t = lax.shift_right_logical(code, 10)
    return t, jnp.minimum(t, 7), lax.bitwise_and(code, 1023)


def first_kernel(
    slot_ref, geo_ref, flux_ref, own_ref, emission_ref, reflect_ref, area_ref,
    leaving_ref, tiles_ref, list_ref, count_ref,
    centre_ref, column_ref, offset_ref, sum_ref, *rest,
):
    bufs, sem = rest[:STEP], rest[STEP]
    prepare_targets(own_ref, centre_ref, column_ref, offset_ref)
    sum_ref[...] = jnp.zeros_like(sum_ref)

    def compact(e, n):
        for k in range(8):
            code = slot_ref[e * 8 + k]
            list_ref[n] = code
            n = n + jnp.where(code >= 0, 1, 0)
        return n

    n = lax.fori_loop(0, slot_ref.shape[0] // 8, compact, 0)
    for k in range(STEP2):
        list_ref[n + k] = 8 << 10
    count_ref[0] = n
    rounds = pl.cdiv(n, STEP)

    def out_copy(i, k):
        side = lax.rem(i, 2)
        to = jnp.minimum(i * STEP + k, KEPT)
        return pltpu.make_async_copy(bufs[k].at[side], tiles_ref.at[to], sem.at[side, k])

    def step(i, carry):
        @pl.when(i >= 2)
        def _():
            for k in range(STEP):
                out_copy(i - 2, k).wait()

        side = lax.rem(i, 2)
        for k in range(STEP):
            t, held, b = decode(list_ref[i * STEP + k])
            build_tile(held, b, geo_ref, centre_ref, column_ref, offset_ref, bufs[k], side)
            add_product(t, block_of(flux_ref, b), bufs[k][side], sum_ref)
        for k in range(STEP):
            out_copy(i, k).start()
        return carry

    lax.fori_loop(0, rounds, step, 0)
    for back in (2, 1):

        @pl.when(rounds >= back)
        def _():
            for k in range(STEP):
                out_copy(rounds - back, k).wait()

    for u in range(16):
        lanes = slice(u * HALF, (u + 1) * HALF)
        radiosity = emission_ref[:, lanes] + reflect_ref[:, lanes] * sum_ref[u // 2, u % 2]
        leaving_ref[u] = (area_ref[:, lanes] * radiosity).astype(jnp.bfloat16)


def second_kernel(
    list_ref, count_ref, geo_ref, flux_ref, own_ref, emission_ref, reflect_ref, tiles_ref,
    out_ref,
    centre_ref, column_ref, offset_ref, sum_ref, spare_ref, buf_ref, sem,
):
    n = count_ref[0]
    sum_ref[...] = jnp.zeros_like(sum_ref)
    rounds = pl.cdiv(jnp.minimum(n, KEPT), STEP2)

    def in_copy(i):
        side = lax.rem(i, 2)
        return pltpu.make_async_copy(
            tiles_ref.at[pl.ds(i * STEP2, STEP2)], buf_ref.at[side], sem.at[side]
        )

    @pl.when(rounds > 0)
    def _():
        in_copy(0).start()

    def step(i, carry):
        @pl.when(i + 1 < rounds)
        def _():
            in_copy(i + 1).start()

        in_copy(i).wait()
        side = lax.rem(i, 2)
        for k in range(STEP2):
            t, held, b = decode(list_ref[i * STEP2 + k])
            add_product(t, block_of(flux_ref, b), buf_ref[side, k], sum_ref)
        return carry

    lax.fori_loop(0, rounds, step, 0)

    @pl.when(n > KEPT)
    def _():
        prepare_targets(own_ref, centre_ref, column_ref, offset_ref)

        def again(e, carry):
            t, held, b = decode(list_ref[e])
            build_tile(held, b, geo_ref, centre_ref, column_ref, offset_ref, spare_ref, 0)
            add_product(t, block_of(flux_ref, b), spare_ref[0], sum_ref)
            return carry

        lax.fori_loop(KEPT, n, again, 0)

    for u in range(16):
        lanes = slice(u * HALF, (u + 1) * HALF)
        out_ref[:, lanes] = emission_ref[:, lanes] + reflect_ref[:, lanes] * sum_ref[u // 2, u % 2]


def per_device(
    positions, normals, emission, material, area_level, reflect_table, area_table, pair_slots
):
    patches = positions.shape[1]
    units = patches // HALF
    me = lax.axis_index("gx") * lax.axis_size("gy") + lax.axis_index("gy")
    level_hot = (
        area_level[None, :] == jnp.arange(area_table.shape[0], dtype=jnp.int32)[:, None]
    ).astype(jnp.float32)
    area = jnp.sum(level_hot * area_table[:, None], axis=0)[None, :]
    kind_hot = (
        material[None, :] == jnp.arange(reflect_table.shape[0], dtype=jnp.int32)[:, None]
    ).astype(jnp.float32)
    reflect = jnp.dot(jnp.transpose(reflect_table), kind_hot, precision=lax.Precision.HIGHEST)

    def in_units(x):
        return jnp.transpose(x.reshape(x.shape[0], units, HALF), (1, 0, 2))

    row, column = pair_slots[0, :, :, 0], pair_slots[0, :, :, 1]
    full = row >= 0
    peers = row.shape[0]
    codes = jnp.where(full, row * 8 + column, -1).reshape(1, -1).astype(jnp.float32)
    codes = jnp.pad(codes, ((0, 0), (0, patches - codes.shape[1])))
    own_geo = in_units(jnp.concatenate([positions, area, normals, codes], axis=0))
    flux = in_units((area * emission).astype(jnp.bfloat16))
    geo, all_flux = gather_all([own_geo, flux], (GEO_PARTS, FLUX_PARTS), 0)
    blocks = peers * 8
    own_blocks = own_geo.reshape(8, 2, 8, HALF)
    at = me * 2
    served = lax.dynamic_slice(
        geo.reshape(peers, units, 8, HALF), (0, at // HALF, 7, at % HALF), (peers, 1, 1, 2)
    ).reshape(peers, 2).astype(jnp.int32)
    geo = geo.reshape(blocks, 2, 8, HALF)
    peer = jnp.arange(peers, dtype=jnp.int32)[:, None] * 8
    own_list = jnp.where(full, row * 1024 + peer + column, -1)
    served_list = jnp.where(served >= 0, (served % 8) * 1024 + peer + served // 8, -1)
    slots = jnp.concatenate([own_list.reshape(-1), served_list.reshape(-1)])

    vmem = pl.BlockSpec(memory_space=pltpu.VMEM)
    smem = pl.BlockSpec(memory_space=pltpu.SMEM)
    anywhere = pl.BlockSpec(memory_space=pl.ANY)
    scratch = [
        pltpu.VMEM((8, 8, BLK), jnp.float32),
        pltpu.VMEM((8, 3 * BLK, 64), jnp.bfloat16),
        pltpu.VMEM((8, BLK, HALF), jnp.float32),
        pltpu.VMEM((9, 2, BANDS, HALF), jnp.float32),
    ]
    limit = pltpu.CompilerParams(vmem_limit_bytes=48 << 20)
    leaving, tiles, listed, counted = pl.pallas_call(
        first_kernel,
        out_shape=[
            jax.ShapeDtypeStruct((units, BANDS, HALF), jnp.bfloat16),
            jax.ShapeDtypeStruct((KEPT + 8, BLK, BLK), jnp.bfloat16),
            jax.ShapeDtypeStruct((slots.shape[0] + STEP2,), jnp.int32),
            jax.ShapeDtypeStruct((1,), jnp.int32),
        ],
        in_specs=[smem] + [vmem] * 6,
        out_specs=[vmem, anywhere, smem, smem],
        scratch_shapes=scratch
        + [pltpu.VMEM((2, BLK, BLK), jnp.bfloat16)] * STEP
        + [pltpu.SemaphoreType.DMA((2, STEP))],
        compiler_params=limit,
        name="first_sweep",
    )(slots, geo, all_flux.reshape(blocks, 2, BANDS, HALF), own_blocks, emission, reflect, area)
    (all_flux,) = gather_all([leaving], (FLUX_PARTS,), 1)
    return pl.pallas_call(
        second_kernel,
        out_shape=jax.ShapeDtypeStruct((BANDS, patches), jnp.float32),
        in_specs=[smem, smem] + [vmem] * 5 + [anywhere],
        out_specs=vmem,
        scratch_shapes=scratch
        + [
            pltpu.VMEM((1, BLK, BLK), jnp.bfloat16),
            pltpu.VMEM((2, STEP2, BLK, BLK), jnp.bfloat16),
            pltpu.SemaphoreType.DMA((2,)),
        ],
        compiler_params=limit,
        name="second_sweep",
    )(
        listed, counted, geo, all_flux.reshape(blocks, 2, BANDS, HALF), own_blocks,
        emission, reflect, tiles,
    )


def solution(mesh):
    placed = (
        P(None, AXES),
        P(None, AXES),
        P(None, AXES),
        P(AXES),
        P(AXES),
        P(),
        P(),
        P(AXES, None, None, None),
    )
    return jax.shard_map(
        per_device, mesh=mesh, in_specs=placed, out_specs=P(None, AXES), check_vma=False
    )
```

time: 666 us -> 229 us (0.34)
  matrix products: 432 us -> 0.95 us
  Pallas kernels: 0 us -> 216 us
  waiting for transfers between devices: 117 us -> 0 us
  local copies, waits for them, and re-layouts: 70 us -> 5.79 us
  starting transfers between devices: 38.5 us -> 0 us
    dot_general x36 -> x0, matrix products: 431 us -> none  [the longest x16 213 us: one_group(): jnp.einsum('sbi,sij->sbj', row_flux, tiles, preferred_element_type=jnp.fl...]
    pallas_call x0 -> x4, Pallas kernels: none -> 216 us  [the longest x2 97.5 us: gather_all(): pl.pallas_call(functools.partial(gather_kernel, parts, count), out_shape=...]
    all_to_all x6 -> x0, waiting for transfers between devices: 117 us -> none  [the longest x2 43.8 us: move_back(): lax.all_to_all(blocks.astype(jnp.bfloat16), ('gx', 'gy'), split_axis=0, c...]
    all_to_all x6 -> x0, starting transfers between devices: 38.5 us -> none  [the longest x1 11.5 us: per_device(): lax.all_to_all(col_local, ('gx', 'gy'), split_axis=0, concat_axis=0, tile...]
    unnamed x60 -> x14, local copies, waits for them, and re-layouts: 21.1 us -> 2.37 us
    gather x7 -> x0, local copies, waits for them, and re-layouts: 17 us -> none  [the longest x2 6.16 us: per_device(): requested_geo = geo_blocks[served_block]]
    squeeze x16 -> x1, local copies, waits for them, and re-layouts: 15.9 us -> 0.14 us  [per_device(): row, column = (pair_slots[0, :, :, 0], pair_slots[0, :, :, 1])]
  transfers between devices with their start and end apart: 6 -> 0, of which waited for: 6 -> 0; matrix products, arithmetic and copies ran while one was open for 6% -> 0% of each run, Pallas kernels for 0% -> 0%
where the time goes in v1:
time: 229 us; the launch traced here: 227 us
  Pallas kernels  216 us (94%)
  local copies, waits for them, and re-layouts  5.79 us (3%)
  other arithmetic  3.83 us (2%)
    pallas_call x2, Pallas kernels, gather_all(): pl.pallas_call(functools.partial(gather_kernel, parts, count), out_shape=...  97.5 us
    pallas_call x1, Pallas kernels, per_device(): pl.pallas_call(first_kernel, out_shape=[jax.ShapeDtypeStruct((units, BAND...  84 us
    pallas_call x1, Pallas kernels, per_device(): pl.pallas_call(second_kernel, out_shape=jax.ShapeDtypeStruct((BANDS, patc...  34.6 us

profile of v1, /device:TPU:1, one launch (start us, length us, event | category | flops | bytes accessed | tf_op | source)
XLA Modules:
  0.0 226.8 jit_solution(18043363650141755726)
XLA Ops:
  0.0 0.0 copy-start
  0.0 0.8 fusion.5
  0.8 0.8 select_reduce_fusion
  1.6 0.1 copy.22
  1.7 0.1 ge.21
  1.9 0.1 copy.23
  2.0 0.1 mul.62
  2.1 0.1 copy.25
  2.3 0.1 squeeze.4
  2.4 0.1 add.67
  2.5 0.2 add.68
  2.6 1.5 bitcast_bitcast_fusion.refs_1_
  4.2 0.1 copy.26
  4.3 0.1 convert_element_type.29
  4.4 1.4 pad_maximum_fusion
  5.9 0.0 copy-done
  5.9 0.9 convolution_bitcast_fusion.reflect_ref
  6.8 54.1 %gather_all.2 = (f32[4,4,4,2,16,8,128]{6,5,4,3,2,1,0:T(8,128)}, bf16[4,4,4,2,16,16,128]{6,5,4,3,2,1,0:T(8,128)(2,1)}) custom-call(f32[16,8,128]{2,1,0:T(8,128)} %bitcast.46, bf16[16,16,128]{2,1,0:T(8,128)(2,1)} %bitcast_bitcast_fusion.refs_1_), custom_call_target="tpu_custom_call" | custom-call | tf_op jit(solution)/shard_map/gather_all/pallas_call | solution.py:149
  60.9 1.2 constant_dynamic-slice_fusion
  62.2 0.1 convert_element_type.32
  62.4 0.0 copy-start.2
  62.4 0.9 copy-done.2
  63.3 0.0 copy-start.4
  63.3 0.8 copy-done.4
  64.1 84.0 %first_sweep.1 = (bf16[16,16,128]{2,1,0:T(8,128)(2,1)S(1)}, bf16[344,256,256]{2,1,0:T(8,128)(2,1)}, s32[520]{0:T(1024)S(1)}, s32[1]{0:T(128)}) custom-call(s32[512]{0:T(512)S(1)} %pad_add_fusion.slot_ref, f32[1024,2,8,128]{3,2,1,0:T(8,128)} %bitcast.52, bf16[1024,2,16,128]{3,2,1,0:T(8,128)(2,1)} %bitcast.55, f32[8,2,8,128]{3,2,1,0:T(8,128)S(1)} %bitcast.47, ...), custom_call_target="tpu_custom_call" | custom-call | tf_op jit(solution)/shard_map/first_sweep/pallas_call | solution.py:413
  148.1 0.0 copy-start.6
  148.2 0.6 copy-done.6
  148.8 0.0 copy-start.3
  148.8 0.0 copy-start.5
  148.8 43.4 %gather_all.3 = bf16[4,4,4,2,16,16,128]{6,5,4,3,2,1,0:T(8,128)(2,1)} custom-call(bf16[16,16,128]{2,1,0:T(8,128)(2,1)} %copy-done.6), custom_call_target="tpu_custom_call" | custom-call | tf_op jit(solution)/shard_map/gather_all/pallas_call | solution.py:149
  192.2 0.0 copy-done.3
  192.2 0.0 copy-done.5
  192.2 0.0 copy-start.1
  192.2 34.6 %second_sweep.1 = f32[16,2048]{1,0:T(8,128)} custom-call(s32[520]{0:T(1024)S(1)} %get-tuple-element.13.list_ref, s32[1]{0:T(128)} %get-tuple-element.14.count_ref, f32[1024,2,8,128]{3,2,1,0:T(8,128)} %bitcast.53, bf16[1024,2,16,128]{3,2,1,0:T(8,128)(2,1)} %bitcast.54, f32[8,2,8,128]{3,2,1,0:T(8,128)S(1)} %bitcast.48, f32[16,2048]{1,0:T(8,128)S(1)} %copy-done.3, ...), custom_call_target="tpu_custom_call" | custom-call | tf_op jit(solution)/shard_map/second_sweep/pallas_call | solution.py:430
  226.8 0.0 copy-done.1
  (7 shorter events, 0.1 us)
Async XLA Ops:
  0.0 5.9 %copy-start = (f32[8,16]{1,0:T(8,128)S(1)}, f32[8,16]{1,0:T(8,128)}, u32[]{:S(2)}) copy-start(f32[8,16]{1,0:T(8,128)} %param.13) | copy-start | bytes 1540
  62.4 0.9 copy-start.2
  63.3 0.8 copy-start.4
  148.1 0.6 copy-start.6
  148.8 43.4 %copy-start.3 = (f32[16,2048]{1,0:T(8,128)S(1)}, f32[16,2048]{1,0:T(8,128)}, u32[]{:S(2)}) copy-start(f32[16,2048]{1,0:T(8,128)} %emission_ref.3) | copy-start | bytes 393220
  148.8 43.4 %copy-start.5 = (f32[8,16,128]{2,0,1:T(8,128)S(1)}, f32[8,16,128]{2,0,1:T(8,128)}, u32[]{:S(2)}) copy-start(f32[8,16,128]{2,0,1:T(8,128)} %pad_maximum_fusion) | copy-start | bytes 196612
  192.2 34.6 %copy-start.1 = (f32[8,16]{1,0:T(8,128)S(1)}, f32[8,16]{1,0:T(8,128)}, u32[]{:S(2)}) copy-start(f32[8,16]{1,0:T(8,128)} %param.13) | copy-start | bytes 1540

commit v2 on v1

--- a/solution.py
+++ b/solution.py
@@ -19,9 +19,11 @@
 FLUX_PARTS = (6, 5, 5)
 GEO_PARTS = (5, 6, 5)
 KEPT = 336
-STEP = 4
+STEP = 8
 STEP2 = 8
 CHUNK = 64
+DEPTH = 4
+SKIP = 8 << 10
 KAPPA = (math.pi - 1.0) / math.pi
 
 
@@ -257,13 +259,20 @@
 
 
 def first_kernel(
-    slot_ref, geo_ref, flux_ref, own_ref, emission_ref, reflect_ref, area_ref,
+    slot_ref, geo_all, flux_all, own_ref, emission_ref, reflect_ref, area_ref,
     leaving_ref, tiles_ref, list_ref, count_ref,
-    centre_ref, column_ref, offset_ref, sum_ref, *rest,
+    geo_ref, flux_ref, load_sem, centre_ref, column_ref, offset_ref, sum_ref, *rest,
 ):
     bufs, sem = rest[:STEP], rest[STEP]
+    loads = [
+        pltpu.make_async_copy(geo_all, geo_ref, load_sem.at[0]),
+        pltpu.make_async_copy(flux_all, flux_ref, load_sem.at[1]),
+    ]
+    for load in loads:
+        load.start()
     prepare_targets(own_ref, centre_ref, column_ref, offset_ref)
     sum_ref[...] = jnp.zeros_like(sum_ref)
+    bufs[-1][1] = jnp.zeros_like(bufs[-1][1])
 
     def compact(e, n):
         for k in range(8):
@@ -274,14 +283,20 @@
 
     n = lax.fori_loop(0, slot_ref.shape[0] // 8, compact, 0)
     for k in range(STEP2):
-        list_ref[n + k] = 8 << 10
+        list_ref[n + k] = SKIP
     count_ref[0] = n
     rounds = pl.cdiv(n, STEP)
+    for load in loads:
+        load.wait()
 
     def out_copy(i, k):
         side = lax.rem(i, 2)
         to = jnp.minimum(i * STEP + k, KEPT)
         return pltpu.make_async_copy(bufs[k].at[side], tiles_ref.at[to], sem.at[side, k])
+
+    def add_tile(code, k, side):
+        t, held, b = decode(code)
+        add_product(t, block_of(flux_ref, b), bufs[k][side], sum_ref)
 
     def step(i, carry):
         @pl.when(i >= 2)
@@ -290,15 +305,23 @@
                 out_copy(i - 2, k).wait()
 
         side = lax.rem(i, 2)
+        before = jnp.where(i > 0, list_ref[jnp.maximum(i * STEP - 1, 0)], SKIP)
         for k in range(STEP):
-            t, held, b = decode(list_ref[i * STEP + k])
+            code = list_ref[i * STEP + k]
+            t, held, b = decode(code)
             build_tile(held, b, geo_ref, centre_ref, column_ref, offset_ref, bufs[k], side)
-            add_product(t, block_of(flux_ref, b), bufs[k][side], sum_ref)
+            if k == 0:
+                add_tile(before, STEP - 1, 1 - side)
+            else:
+                add_tile(before, k - 1, side)
+            before = code
         for k in range(STEP):
             out_copy(i, k).start()
         return carry
 
     lax.fori_loop(0, rounds, step, 0)
+    last = jnp.where(rounds > 0, list_ref[jnp.maximum(rounds * STEP - 1, 0)], SKIP)
+    add_tile(last, STEP - 1, lax.rem(rounds + 1, 2))
     for back in (2, 1):
 
         @pl.when(rounds >= back)
@@ -313,31 +336,37 @@
 
 
 def second_kernel(
-    list_ref, count_ref, geo_ref, flux_ref, own_ref, emission_ref, reflect_ref, tiles_ref,
+    list_ref, count_ref, geo_all, flux_all, own_ref, emission_ref, reflect_ref, tiles_ref,
     out_ref,
-    centre_ref, column_ref, offset_ref, sum_ref, spare_ref, buf_ref, sem,
+    geo_ref, flux_ref, load_sem, centre_ref, column_ref, offset_ref, sum_ref, spare_ref, buf_ref, sem,
 ):
     n = count_ref[0]
-    sum_ref[...] = jnp.zeros_like(sum_ref)
     rounds = pl.cdiv(jnp.minimum(n, KEPT), STEP2)
 
     def in_copy(i):
-        side = lax.rem(i, 2)
+        side = lax.rem(i, DEPTH)
         return pltpu.make_async_copy(
             tiles_ref.at[pl.ds(i * STEP2, STEP2)], buf_ref.at[side], sem.at[side]
         )
 
-    @pl.when(rounds > 0)
-    def _():
-        in_copy(0).start()
+    load = pltpu.make_async_copy(flux_all, flux_ref, load_sem.at[1])
+    load.start()
+    for i in range(DEPTH - 1):
+
+        @pl.when(i < rounds)
+        def _():
+            in_copy(i).start()
+
+    sum_ref[...] = jnp.zeros_like(sum_ref)
+    load.wait()
 
     def step(i, carry):
-        @pl.when(i + 1 < rounds)
+        @pl.when(i + DEPTH - 1 < rounds)
         def _():
-            in_copy(i + 1).start()
+            in_copy(i + DEPTH - 1).start()
 
         in_copy(i).wait()
-        side = lax.rem(i, 2)
+        side = lax.rem(i, DEPTH)
         for k in range(STEP2):
             t, held, b = decode(list_ref[i * STEP2 + k])
             add_product(t, block_of(flux_ref, b), buf_ref[side, k], sum_ref)
@@ -347,6 +376,9 @@
 
     @pl.when(n > KEPT)
     def _():
+        again_load = pltpu.make_async_copy(geo_all, geo_ref, load_sem.at[0])
+        again_load.start()
+        again_load.wait()
         prepare_targets(own_ref, centre_ref, column_ref, offset_ref)
 
         def again(e, carry):
@@ -404,6 +436,9 @@
     smem = pl.BlockSpec(memory_space=pltpu.SMEM)
     anywhere = pl.BlockSpec(memory_space=pl.ANY)
     scratch = [
+        pltpu.VMEM((blocks, 2, 8, HALF), jnp.float32),
+        pltpu.VMEM((blocks, 2, BANDS, HALF), jnp.bfloat16),
+        pltpu.SemaphoreType.DMA((2,)),
         pltpu.VMEM((8, 8, BLK), jnp.float32),
         pltpu.VMEM((8, 3 * BLK, 64), jnp.bfloat16),
         pltpu.VMEM((8, BLK, HALF), jnp.float32),
@@ -418,7 +453,7 @@
             jax.ShapeDtypeStruct((slots.shape[0] + STEP2,), jnp.int32),
             jax.ShapeDtypeStruct((1,), jnp.int32),
         ],
-        in_specs=[smem] + [vmem] * 6,
+        in_specs=[smem, anywhere, anywhere] + [vmem] * 4,
         out_specs=[vmem, anywhere, smem, smem],
         scratch_shapes=scratch
         + [pltpu.VMEM((2, BLK, BLK), jnp.bfloat16)] * STEP
@@ -430,13 +465,13 @@
     return pl.pallas_call(
         second_kernel,
         out_shape=jax.ShapeDtypeStruct((BANDS, patches), jnp.float32),
-        in_specs=[smem, smem] + [vmem] * 5 + [anywhere],
+        in_specs=[smem, smem, anywhere, anywhere] + [vmem] * 3 + [anywhere],
         out_specs=vmem,
         scratch_shapes=scratch
         + [
             pltpu.VMEM((1, BLK, BLK), jnp.bfloat16),
-            pltpu.VMEM((2, STEP2, BLK, BLK), jnp.bfloat16),
-            pltpu.SemaphoreType.DMA((2,)),
+            pltpu.VMEM((DEPTH, STEP2, BLK, BLK), jnp.bfloat16),
+            pltpu.SemaphoreType.DMA((DEPTH,)),
         ],
         compiler_params=limit,
         name="second_sweep",

time: 229 us -> 175 us (0.76)
  Pallas kernels: 216 us -> 164 us
    pallas_call x1, Pallas kernels: 84 us -> 49.3 us  [per_device(): pl.pallas_call(first_kernel, out_shape=[jax.ShapeDtypeStruct((units, BAND...]
    pallas_call x1, Pallas kernels: 34.6 us -> 20.5 us  [per_device(): pl.pallas_call(second_kernel, out_shape=jax.ShapeDtypeStruct((BANDS, patc...]
    pallas_call x2, Pallas kernels: 97.5 us -> 93.7 us  [gather_all(): pl.pallas_call(functools.partial(gather_kernel, parts, count), out_shape=...]
where the time goes in v2:
time: 175 us; the launch traced here: 174 us
  Pallas kernels  164 us (94%)
  local copies, waits for them, and re-layouts  5.79 us (3%)
  other arithmetic  3.83 us (2%)
    pallas_call x2, Pallas kernels, gather_all(): pl.pallas_call(functools.partial(gather_kernel, parts, count), out_shape=...  93.7 us
    pallas_call x1, Pallas kernels, per_device(): pl.pallas_call(first_kernel, out_shape=[jax.ShapeDtypeStruct((units, BAND...  49.3 us
    pallas_call x1, Pallas kernels, per_device(): pl.pallas_call(second_kernel, out_shape=jax.ShapeDtypeStruct((BANDS, patc...  20.5 us

profile of v2, /device:TPU:1, one launch (start us, length us, event | category | flops | bytes accessed | tf_op | source)
XLA Modules:
  0.0 174.3 jit_solution(4639172339481446572)
XLA Ops:
  0.0 0.0 copy-start
  0.0 0.8 fusion.5
  0.8 0.8 select_reduce_fusion
  1.6 0.1 copy.22
  1.7 0.1 ge.21
  1.9 0.1 copy.23
  2.0 0.1 mul.62
  2.1 0.1 copy.25
  2.3 0.1 squeeze.4
  2.4 0.1 add.67
  2.5 0.2 add.68
  2.6 1.5 bitcast_bitcast_fusion.refs_1_
  4.2 0.1 copy.26
  4.3 0.1 convert_element_type.29
  4.4 1.4 pad_maximum_fusion
  5.9 0.0 copy-done
  5.9 0.9 convolution_bitcast_fusion.reflect_ref
  6.8 54.1 %gather_all.2 = (f32[4,4,4,2,16,8,128]{6,5,4,3,2,1,0:T(8,128)}, bf16[4,4,4,2,16,16,128]{6,5,4,3,2,1,0:T(8,128)(2,1)}) custom-call(f32[16,8,128]{2,1,0:T(8,128)} %bitcast.46, bf16[16,16,128]{2,1,0:T(8,128)(2,1)} %bitcast_bitcast_fusion.refs_1_), custom_call_target="tpu_custom_call" | custom-call | tf_op jit(solution)/shard_map/gather_all/pallas_call | solution.py:151
  60.9 1.2 constant_dynamic-slice_fusion
  62.2 0.1 convert_element_type.32
  62.4 0.0 copy-start.2
  62.4 0.9 copy-done.2
  63.3 0.0 copy-start.4
  63.3 0.8 copy-done.4
  64.1 49.3 %first_sweep.1 = (bf16[16,16,128]{2,1,0:T(8,128)(2,1)S(1)}, bf16[344,256,256]{2,1,0:T(8,128)(2,1)}, s32[520]{0:T(1024)S(1)}, s32[1]{0:T(128)}) custom-call(s32[512]{0:T(512)S(1)} %pad_add_fusion.slot_ref, f32[1024,2,8,128]{3,2,1,0:T(8,128)} %bitcast.52, bf16[1024,2,16,128]{3,2,1,0:T(8,128)(2,1)} %bitcast.55, f32[8,2,8,128]{3,2,1,0:T(8,128)S(1)} %bitcast.47, ...), custom_call_target="tpu_custom_call" | custom-call | tf_op jit(solution)/shard_map/first_sweep/pallas_call | solution.py:448
  113.4 0.0 copy-start.6
  113.4 0.6 copy-done.6
  114.0 0.0 copy-start.3
  114.0 0.0 copy-start.5
  114.0 39.7 %gather_all.3 = bf16[4,4,4,2,16,16,128]{6,5,4,3,2,1,0:T(8,128)(2,1)} custom-call(bf16[16,16,128]{2,1,0:T(8,128)(2,1)} %copy-done.6), custom_call_target="tpu_custom_call" | custom-call | tf_op jit(solution)/shard_map/gather_all/pallas_call | solution.py:151
  153.7 0.0 copy-done.3
  153.7 0.0 copy-done.5
  153.7 0.0 copy-start.1
  153.7 20.5 %second_sweep.1 = f32[16,2048]{1,0:T(8,128)} custom-call(s32[520]{0:T(1024)S(1)} %get-tuple-element.13.list_ref, s32[1]{0:T(128)} %get-tuple-element.14.count_ref, f32[1024,2,8,128]{3,2,1,0:T(8,128)} %bitcast.53, bf16[1024,2,16,128]{3,2,1,0:T(8,128)(2,1)} %bitcast.54, f32[8,2,8,128]{3,2,1,0:T(8,128)S(1)} %bitcast.48, f32[16,2048]{1,0:T(8,128)S(1)} %copy-done.3, ...), custom_call_target="tpu_custom_call" | custom-call | tf_op jit(solution)/shard_map/second_sweep/pallas_call | solution.py:465
  174.3 0.0 copy-done.1
  (7 shorter events, 0.1 us)
Async XLA Ops:
  0.0 5.9 %copy-start = (f32[8,16]{1,0:T(8,128)S(1)}, f32[8,16]{1,0:T(8,128)}, u32[]{:S(2)}) copy-start(f32[8,16]{1,0:T(8,128)} %param.13) | copy-start | bytes 1540
  62.4 0.9 copy-start.2
  63.3 0.8 copy-start.4
  113.4 0.6 copy-start.6
  114.0 39.7 %copy-start.3 = (f32[16,2048]{1,0:T(8,128)S(1)}, f32[16,2048]{1,0:T(8,128)}, u32[]{:S(2)}) copy-start(f32[16,2048]{1,0:T(8,128)} %emission_ref.3) | copy-start | bytes 393220
  114.0 39.7 %copy-start.5 = (f32[8,16,128]{2,0,1:T(8,128)S(1)}, f32[8,16,128]{2,0,1:T(8,128)}, u32[]{:S(2)}) copy-start(f32[8,16,128]{2,0,1:T(8,128)} %pad_maximum_fusion) | copy-start | bytes 196612
  153.7 20.5 %copy-start.1 = (f32[8,16]{1,0:T(8,128)S(1)}, f32[8,16]{1,0:T(8,128)}, u32[]{:S(2)}) copy-start(f32[8,16]{1,0:T(8,128)} %param.13) | copy-start | bytes 1540

commit v3 on v2

v3 whole, which is shorter than its diff:
```python
import functools
import math

import jax
import jax.numpy as jnp
from jax import lax
from jax.experimental import pallas as pl
from jax.experimental.pallas import tpu as pltpu
from jax.sharding import PartitionSpec as P

MESH = pl.DeviceIdType.MESH
BANDS = 16
BLK = 256
HALF = 128
ITERS = 2
AXES = ("gx", "gy")
SIDE = 4
ORDERS = (("x", "y", "z"), ("y", "z", "x"), ("z", "x", "y"))
FIRST_PARTS = (((0, 11), (1, 5)), ((1, 6), (2, 10)))
LATER_PARTS = (((0, 6), (1, 5), (2, 5)),)
KEPT = 336
STEP = 8
STEP2 = 8
CHUNK = 64
DEPTH = 4
SKIP = 8 << 10
KAPPA = (math.pi - 1.0) / math.pi


def my_place():
    z = lax.axis_index("gx")
    inner = lax.axis_index("gy")
    place = {"z": z, "y": lax.div(inner, 2 * SIDE), "x": lax.rem(lax.div(inner, 2), SIDE)}
    return place, lax.rem(inner, 2)


def device_of(place, core):
    return (place["z"], (place["y"] * SIDE + place["x"]) * 2 + core)


def moved(place, axis, by):
    other = dict(place)
    other[axis] = lax.rem(place[axis] + (by + SIDE), SIDE)
    return other


def own_first(refs, srcs):
    position_ref, normal_ref, emission_ref, level_ref, area_ref, slot_ref = refs
    geo_ref, flux_ref = srcs
    for u in range(position_ref.shape[1] // HALF):
        lanes = slice(u * HALF, (u + 1) * HALF)
        level = level_ref[:, lanes]
        area = jnp.zeros(level.shape, jnp.float32)
        for m in range(area_ref.shape[0]):
            area = jnp.where(level == m, area_ref[m], area)
        code = jnp.zeros(area.shape, jnp.float32)
        if u < 2:
            row, column = slot_ref[u, 0:1, :], slot_ref[u, 1:2, :]
            code = jnp.where(row >= 0, row * 8 + column, -1).astype(jnp.float32)
        geo_ref[u] = jnp.concatenate(
            [position_ref[:, lanes], area, normal_ref[:, lanes], code], axis=0
        )
        flux_ref[u] = (area * emission_ref[:, lanes]).astype(jnp.bfloat16)


def gather_kernel(parts, count, prologue, inputs, *refs):
    bufs, rest = refs[inputs : inputs + count], refs[inputs + count :]
    send_sem, recv_sem, local_sem = rest[:3]
    srcs = rest[3:] if prologue else refs[:count]
    here, core = my_place()
    other_core = device_of(here, 1 - core)
    barrier = pltpu.get_barrier_semaphore()
    peers = [device_of(moved(here, axis, by), core) for axis in "zyx" for by in (1, -1, 2)]
    peers.append(other_core)
    for peer in peers:
        pl.semaphore_signal(barrier, inc=1, device_id=peer, device_id_type=MESH)
    if prologue:
        prologue(refs[:inputs], srcs)
    own_copies = []
    for b in range(count):
        place = bufs[b].at[here["z"], here["y"], here["x"], core]
        own_copies.append(pltpu.make_async_copy(srcs[b], place, local_sem.at[b]))
        own_copies[-1].start()
    pl.semaphore_wait(barrier, len(peers))
    started = []
    shared = []

    def send(src, dst, to):
        n = len(started)
        copy = pltpu.make_async_remote_copy(
            src_ref=src,
            dst_ref=dst,
            send_sem=send_sem.at[n],
            recv_sem=recv_sem.at[n],
            device_id=to,
            device_id_type=MESH,
        )
        copy.start()
        started.append(copy)
        return copy

    def view(b, index, first, size):
        return bufs[b].at[index["z"], index["y"], index["x"], core, pl.ds(first, size)]

    def share(b, index, first, size):
        piece = view(b, index, first, size)
        shared.append(send(piece, piece, other_core))

    work = []
    for b in range(count):
        first = 0
        for k, size in parts[b]:
            work.append((b, k, first, size))
            first += size

    for copy in own_copies:
        copy.wait()

    def at(k, line, plane, far):
        index = {}
        for axis, by in zip(ORDERS[k], (line, plane, far)):
            index[axis] = pl.ds(0, SIDE) if by is None else moved(here, axis, by)[axis]
        return index

    def to(k, stage, by):
        return device_of(moved(here, ORDERS[k][stage], by), core)

    def pass_on(item, stage, by, index):
        b, k, first, size = item
        piece = view(b, index, first, size)
        return send(piece, piece, to(k, stage, by))

    def half(k, index, which):
        index = dict(index)
        index[ORDERS[k][0]] = pl.ds(2 * which, 2)
        return index

    line, plane, ahead, far, again = {}, {}, {}, {}, {}
    for item in work:
        b, k, first, size = item
        src, dst = srcs[b].at[pl.ds(first, size)], view(b, here, first, size)
        line[item] = [send(src, dst, to(k, 0, by)) for by in (1, -1, 2)]
    for item in work:
        b, k, first, size = item
        for copy in line[item]:
            copy.wait_recv()
        mine = at(k, None, 0, 0)
        plane[item] = {by: pass_on(item, 1, by, mine) for by in (1, -1)}
        for by in (1, -1):
            far[item, 0, by] = pass_on(item, 2, by, mine)
        share(b, mine, first, size)
    for item in work:
        b, k, first, size = item
        plane[item][1].wait_recv()
        up = pass_on(item, 1, 1, half(k, at(k, None, -1, 0), 0))
        plane[item][-1].wait_recv()
        down = pass_on(item, 1, -1, half(k, at(k, None, 1, 0), 1))
        ahead[item] = [up, down]
        for row in (-1, 1):
            index = at(k, None, row, 0)
            for by in (1, -1):
                far[item, row, by] = pass_on(item, 2, by, index)
            share(b, index, first, size)

    def forward(item, row):
        k = item[1]
        far[item, row, 1].wait_recv()
        up = pass_on(item, 2, 1, half(k, at(k, None, row, -1), 0))
        far[item, row, -1].wait_recv()
        down = pass_on(item, 2, -1, half(k, at(k, None, row, 1), 1))
        again[item, row] = [up, down]

    def share_far(item, row):
        b, k, first, size = item
        share(b, at(k, None, row, -1), first, size)
        share(b, at(k, None, row, 1), first, size)

    for item in work:
        forward(item, 0)
        share_far(item, 0)
    for item in work:
        b, k, first, size = item
        for copy in ahead[item]:
            copy.wait_recv()
        index = at(k, None, 2, 0)
        for by in (1, -1):
            far[item, 2, by] = pass_on(item, 2, by, index)
        share(b, index, first, size)
    for row in (-1, 1, 2):
        for item in work:
            forward(item, row)
            share_far(item, row)
    for row in (0, -1, 1, 2):
        for item in work:
            b, k, first, size = item
            for copy in again[item, row]:
                copy.wait_recv()
            if row == 1:
                pass
            share(b, at(k, None, row, 2), first, size)
    for copy in shared:
        copy.wait_recv()
    for copy in started:
        copy.wait_send()


def gather_all(shapes, parts, collective_id, specs, inputs, prologue=None):
    count = len(shapes)
    copies = 39 * sum(len(p) for p in parts)
    own = [pltpu.VMEM(a.shape, a.dtype) for a in shapes] if prologue else []
    return pl.pallas_call(
        functools.partial(gather_kernel, parts, count, prologue, len(inputs)),
        out_shape=[
            jax.ShapeDtypeStruct((SIDE, SIDE, SIDE, 2) + a.shape, a.dtype) for a in shapes
        ],
        in_specs=specs,
        out_specs=[pl.BlockSpec(memory_space=pl.ANY)] * count,
        scratch_shapes=[
            pltpu.SemaphoreType.DMA((copies,)),
            pltpu.SemaphoreType.DMA((copies,)),
            pltpu.SemaphoreType.DMA((count,)),
        ]
        + own,
        compiler_params=pltpu.CompilerParams(
            collective_id=collective_id, has_side_effects=True, vmem_limit_bytes=2 << 20
        ),
        name="gather_all",
    )(*inputs)


def my_block():
    return (lax.axis_index("gx") * lax.axis_size("gy") + lax.axis_index("gy")) * 8


def reflect_of(table_ref, material_ref, lanes):
    material = material_ref[:, lanes]
    kinds = table_ref.shape[0]
    hot = lax.broadcasted_iota(jnp.int32, (kinds, HALF), 0) == material
    return lax.dot_general(
        table_ref[...],
        jnp.where(hot, 1.0, 0.0),
        (((0,), (0,)), ((), ())),
        precision=lax.Precision.HIGHEST,
        preferred_element_type=jnp.float32,
    )


def split3(x):
    a = x.astype(jnp.bfloat16).astype(jnp.float32)
    rest = x - a
    b = rest.astype(jnp.bfloat16).astype(jnp.float32)
    return a, b, rest - b


def block_of(ref, b):
    return jnp.concatenate([ref[b, 0], ref[b, 1]], axis=1)


def centred(rows, centre):
    moved_rows = rows - centre
    squares = moved_rows * moved_rows
    cross = moved_rows * pltpu.roll(moved_rows, 4, 0)
    reach = (squares[0:1] + squares[1:2] + squares[2:3]) + 0.5 * rows[3:4]
    plane = -(cross[0:1] + cross[1:2] + cross[2:3])
    return moved_rows, reach, plane


def source_rows(rows, centre):
    at = lax.broadcasted_iota(jnp.int32, rows.shape, 0)
    base, reach, plane = centred(rows, centre)
    base = jnp.where(at == 3, reach, jnp.where(at == 7, plane, base))
    a, b, c = split3(base)
    one = jnp.where(at < 3, 1.0, 0.0)
    stacked = jnp.concatenate([a, a, a, b, b, c, one, jnp.zeros_like(one)], axis=0)
    return stacked.astype(jnp.bfloat16), (KAPPA * 0.5) * rows[3:4]


def target_columns(rows, centre):
    at = lax.broadcasted_iota(jnp.int32, rows.shape, 0)
    base, reach, plane = centred(rows, centre)
    zero = jnp.zeros_like(base)
    swapped = pltpu.roll(base, 4, 0)
    facing = jnp.where(at < 3, swapped, 0.0) * (1.0 / math.pi)
    seen = jnp.where((at >= 4) & (at < 7), swapped, jnp.where(at == 7, 1.0, 0.0))
    spread = jnp.where(at < 3, -2.0 * base, jnp.where(at == 3, 1.0, 0.0))
    columns = []
    for factor, constant in ((facing, plane * (1.0 / math.pi)), (seen, None), (spread, reach)):
        a, b, c = split3(factor)
        last = zero
        if constant is not None:
            d, e, f = split3(constant)
            last = jnp.where(at == 0, d, jnp.where(at == 1, e, jnp.where(at == 2, f, 0.0)))
        stacked = jnp.concatenate([a, b, c, a, b, a, last, zero], axis=0)
        columns.append(jnp.transpose(stacked).astype(jnp.bfloat16))
    return columns, (KAPPA * 0.5) * rows[3:4]


def prepare_targets(geo_ref, centre_ref, column_ref, offset_ref):
    for t in range(8):
        rows = block_of(geo_ref, my_block() + t)
        at = lax.broadcasted_iota(jnp.int32, rows.shape, 0)
        centre = jnp.where(at < 3, jnp.broadcast_to(rows[:, 0:1], rows.shape), 0.0)
        centre_ref[t] = centre
        columns, offset = target_columns(rows, centre)
        for r in range(0, BLK, CHUNK):
            column_ref[t, 3 * r : 3 * (r + CHUNK)] = jnp.concatenate(
                [c[r : r + CHUNK] for c in columns], axis=0
            )
        offset_ref[t] = jnp.transpose(jnp.broadcast_to(offset, (HALF, BLK)))


def build_tile(t, b, geo_ref, centre_ref, column_ref, offset_ref, tile_ref, slot):
    source, source_offset = source_rows(block_of(geo_ref, b), centre_ref[t])
    for r in range(0, BLK, CHUNK):
        terms = jnp.dot(
            column_ref[t, 3 * r : 3 * (r + CHUNK), :], source, preferred_element_type=jnp.float32
        )
        facing, seen, spread = terms[:CHUNK], terms[CHUNK : 2 * CHUNK], terms[2 * CHUNK :]
        offset = offset_ref[t, r : r + CHUNK, :]
        offset = jnp.concatenate([offset, offset], axis=1)
        over = jnp.maximum(facing, 0.0) * jnp.maximum(seen, 0.0)
        under = spread * ((spread - offset) - source_offset)
        inverse = pl.reciprocal(under, approx=True)
        inverse = inverse * (2.0 - under * inverse)
        tile_ref[slot, r : r + CHUNK, :] = (over * inverse).astype(jnp.bfloat16)


def add_product(t, flux, tile, sum_ref):
    term = lax.dot_general(
        flux, tile, (((1,), (1,)), ((), ())), preferred_element_type=jnp.float32
    )
    sum_ref[t, 0] += term[:, :HALF]
    sum_ref[t, 1] += term[:, HALF:]


def decode(code):
    t = lax.shift_right_logical(code, 10)
    return t, jnp.minimum(t, 7), lax.bitwise_and(code, 1023)


def first_kernel(
    geo_ref, flux_ref, emission_ref, material_ref, table_ref,
    leaving_ref, tiles_ref, list_ref, count_ref, kept_ref,
    code_ref, entry_ref, slot_ref, slot_sem, centre_ref, column_ref, offset_ref, sum_ref, *rest,
):
    bufs, sem = rest[:STEP], rest[STEP]
    first = my_block()
    peers = geo_ref.shape[0] // 8
    peer = lax.broadcasted_iota(jnp.int32, (1, peers), 1)
    at_me = lax.broadcasted_iota(jnp.int32, (8, HALF), 1) == lax.div(first, 8)
    pick = jnp.where(at_me, 1.0, 0.0).astype(jnp.bfloat16)
    entry_ref[...] = jnp.full_like(entry_ref, -1)
    for c in range(2):
        for p in range(peers):
            code_ref[p : p + 1, :] = geo_ref[p * 8, c, 7:8, :]
        served = lax.dot_general(
            pick,
            code_ref[...].astype(jnp.bfloat16),
            (((1,), (1,)), ((), ())),
            preferred_element_type=jnp.float32,
        )[0:1].astype(jnp.int32)
        owned = geo_ref[first, c, 7:8, :].astype(jnp.int32)
        for row, code, own in ((c, owned, True), (2 + c, served, False)):
            high, low = lax.shift_right_arithmetic(code, 3), lax.bitwise_and(code, 7)
            target, source = (high, low) if own else (low, high)
            entry_ref[row : row + 1, :] = jnp.where(
                code >= 0, target * 1024 + peer * 8 + source, -1
            )
    slot_copy = pltpu.make_async_copy(entry_ref, slot_ref, slot_sem)
    slot_copy.start()
    prepare_targets(geo_ref, centre_ref, column_ref, offset_ref)
    sum_ref[...] = jnp.zeros_like(sum_ref)
    slot_copy.wait()
    bufs[-1][1] = jnp.zeros_like(bufs[-1][1])

    def compact(e, n):
        for k in range(8):
            code = slot_ref[lax.div(e, HALF // 8), lax.rem(e, HALF // 8) * 8 + k]
            list_ref[n] = code
            n = n + jnp.where(code >= 0, 1, 0)
        return n

    n = lax.fori_loop(0, 4 * HALF // 8, compact, 0)
    for k in range(STEP2):
        list_ref[n + k] = SKIP
    count_ref[0] = n

    @pl.when(n > KEPT)
    def _():
        keep = pltpu.make_async_copy(geo_ref, kept_ref, slot_sem)
        keep.start()
        keep.wait()

    rounds = pl.cdiv(n, STEP)

    def out_copy(i, k):
        side = lax.rem(i, 2)
        to = jnp.minimum(i * STEP + k, KEPT)
        return pltpu.make_async_copy(bufs[k].at[side], tiles_ref.at[to], sem.at[side, k])

    def add_tile(code, k, side):
        t, held, b = decode(code)
        add_product(t, block_of(flux_ref, b), bufs[k][side], sum_ref)

    def step(i, carry):
        @pl.when(i >= 2)
        def _():
            for k in range(STEP):
                out_copy(i - 2, k).wait()

        side = lax.rem(i, 2)
        before = jnp.where(i > 0, list_ref[jnp.maximum(i * STEP - 1, 0)], SKIP)
        for k in range(STEP):
            code = list_ref[i * STEP + k]
            t, held, b = decode(code)
            build_tile(held, b, geo_ref, centre_ref, column_ref, offset_ref, bufs[k], side)
            if k == 0:
                add_tile(before, STEP - 1, 1 - side)
            else:
                add_tile(before, k - 1, side)
            before = code
        for k in range(STEP):
            out_copy(i, k).start()
        return carry

    lax.fori_loop(0, rounds, step, 0)
    last = jnp.where(rounds > 0, list_ref[jnp.maximum(rounds * STEP - 1, 0)], SKIP)
    add_tile(last, STEP - 1, lax.rem(rounds + 1, 2))
    for back in (2, 1):

        @pl.when(rounds >= back)
        def _():
            for k in range(STEP):
                out_copy(rounds - back, k).wait()

    for u in range(16):
        lanes = slice(u * HALF, (u + 1) * HALF)
        reflect = reflect_of(table_ref, material_ref, lanes)
        radiosity = emission_ref[:, lanes] + reflect * sum_ref[u // 2, u % 2]
        area = geo_ref[first + u // 2, u % 2, 3:4, :]
        leaving_ref[u] = (area * radiosity).astype(jnp.bfloat16)


def second_kernel(
    list_ref, count_ref, geo_all, flux_ref, emission_ref, material_ref, table_ref, tiles_ref,
    out_ref,
    geo_ref, load_sem, centre_ref, column_ref, offset_ref, sum_ref, spare_ref, buf_ref, sem,
):
    n = count_ref[0]
    rounds = pl.cdiv(jnp.minimum(n, KEPT), STEP2)

    def in_copy(i):
        side = lax.rem(i, DEPTH)
        return pltpu.make_async_copy(
            tiles_ref.at[pl.ds(i * STEP2, STEP2)], buf_ref.at[side], sem.at[side]
        )

    for i in range(DEPTH - 1):

        @pl.when(i < rounds)
        def _():
            in_copy(i).start()

    sum_ref[...] = jnp.zeros_like(sum_ref)

    def step(i, carry):
        @pl.when(i + DEPTH - 1 < rounds)
        def _():
            in_copy(i + DEPTH - 1).start()

        in_copy(i).wait()
        side = lax.rem(i, DEPTH)
        for k in range(STEP2):
            t, held, b = decode(list_ref[i * STEP2 + k])
            add_product(t, block_of(flux_ref, b), buf_ref[side, k], sum_ref)
        return carry

    lax.fori_loop(0, rounds, step, 0)

    @pl.when(n > KEPT)
    def _():
        again_load = pltpu.make_async_copy(geo_all, geo_ref, load_sem)
        again_load.start()
        again_load.wait()
        prepare_targets(geo_ref, centre_ref, column_ref, offset_ref)

        def again(e, carry):
            t, held, b = decode(list_ref[e])
            build_tile(held, b, geo_ref, centre_ref, column_ref, offset_ref, spare_ref, 0)
            add_product(t, block_of(flux_ref, b), spare_ref[0], sum_ref)
            return carry

        lax.fori_loop(KEPT, n, again, 0)

    for u in range(16):
        lanes = slice(u * HALF, (u + 1) * HALF)
        reflect = reflect_of(table_ref, material_ref, lanes)
        out_ref[:, lanes] = emission_ref[:, lanes] + reflect * sum_ref[u // 2, u % 2]


def per_device(
    positions, normals, emission, material, area_level, reflect_table, area_table, pair_slots
):
    patches = positions.shape[1]
    units = patches // HALF
    peers = pair_slots.shape[1]
    blocks = peers * 8
    vmem = pl.BlockSpec(memory_space=pltpu.VMEM)
    smem = pl.BlockSpec(memory_space=pltpu.SMEM)
    anywhere = pl.BlockSpec(memory_space=pl.ANY)
    material, level = material.reshape(1, patches), area_level.reshape(1, patches)
    slots = jnp.transpose(pair_slots[0], (1, 2, 0))
    geo_units = jax.ShapeDtypeStruct((units, 8, HALF), jnp.float32)
    flux_units = jax.ShapeDtypeStruct((units, BANDS, HALF), jnp.bfloat16)
    geo, flux = gather_all(
        [geo_units, flux_units],
        FIRST_PARTS,
        0,
        [vmem] * 4 + [smem, vmem],
        [positions, normals, emission, level, area_table, slots],
        own_first,
    )
    geo = geo.reshape(blocks, 2, 8, HALF)

    scratch = [
        pltpu.VMEM((8, 8, BLK), jnp.float32),
        pltpu.VMEM((8, 3 * BLK, 64), jnp.bfloat16),
        pltpu.VMEM((8, BLK, HALF), jnp.float32),
        pltpu.VMEM((9, 2, BANDS, HALF), jnp.float32),
    ]
    leaving, tiles, listed, counted, kept = pl.pallas_call(
        first_kernel,
        out_shape=[
            jax.ShapeDtypeStruct((units, BANDS, HALF), jnp.bfloat16),
            jax.ShapeDtypeStruct((KEPT + 8, BLK, BLK), jnp.bfloat16),
            jax.ShapeDtypeStruct((4 * peers + STEP2,), jnp.int32),
            jax.ShapeDtypeStruct((1,), jnp.int32),
            jax.ShapeDtypeStruct(geo.shape, jnp.float32),
        ],
        in_specs=[vmem] * 5,
        out_specs=[vmem, anywhere, smem, smem, anywhere],
        scratch_shapes=[
            pltpu.VMEM((peers, HALF), jnp.float32),
            pltpu.VMEM((8, peers), jnp.int32),
            pltpu.SMEM((8, peers), jnp.int32),
            pltpu.SemaphoreType.DMA(()),
        ]
        + scratch
        + [pltpu.VMEM((2, BLK, BLK), jnp.bfloat16)] * STEP
        + [pltpu.SemaphoreType.DMA((2, STEP))],
        compiler_params=pltpu.CompilerParams(vmem_limit_bytes=14 << 20),
        name="first_sweep",
    )(geo, flux.reshape(blocks, 2, BANDS, HALF), emission, material, reflect_table)
    (flux,) = gather_all([flux_units], LATER_PARTS, 1, [anywhere], [leaving])
    return pl.pallas_call(
        second_kernel,
        out_shape=jax.ShapeDtypeStruct((BANDS, patches), jnp.float32),
        in_specs=[smem, smem, anywhere] + [vmem] * 4 + [anywhere],
        out_specs=vmem,
        scratch_shapes=[
            pltpu.VMEM((blocks, 2, 8, HALF), jnp.float32),
            pltpu.SemaphoreType.DMA(()),
        ]
        + scratch
        + [
            pltpu.VMEM((1, BLK, BLK), jnp.bfloat16),
            pltpu.VMEM((DEPTH, STEP2, BLK, BLK), jnp.bfloat16),
            pltpu.SemaphoreType.DMA((DEPTH,)),
        ],
        compiler_params=pltpu.CompilerParams(vmem_limit_bytes=22 << 20),
        name="second_sweep",
    )(
        listed, counted, kept, flux.reshape(blocks, 2, BANDS, HALF), emission, material,
        reflect_table, tiles,
    )


def solution(mesh):
    placed = (
        P(None, AXES),
        P(None, AXES),
        P(None, AXES),
        P(AXES),
        P(AXES),
        P(),
        P(),
        P(AXES, None, None, None),
    )
    return jax.shard_map(
        per_device, mesh=mesh, in_specs=placed, out_specs=P(None, AXES), check_vma=False
    )
```

time: 175 us -> 152 us (0.87)
  Pallas kernels: 164 us -> 144 us
  other arithmetic: 3.83 us -> 0 us
    pallas_call x2, Pallas kernels: 93.7 us -> 79.1 us  [gather_all(): pl.pallas_call(functools.partial(gather_kernel, parts, count, prologue, l...]
    unnamed x14 -> x22, local copies, waits for them, and re-layouts: 2.37 us -> 6.75 us
    pallas_call x1, Pallas kernels: 49.3 us -> 46.9 us  [per_device(): pl.pallas_call(first_kernel, out_shape=[jax.ShapeDtypeStruct((units, BAND...]
    pallas_call x1, Pallas kernels: 20.5 us -> 18.5 us  [per_device(): pl.pallas_call(second_kernel, out_shape=jax.ShapeDtypeStruct((BANDS, patc...]
where the time goes in v3:
time: 152 us; the launch traced here: 151 us
  Pallas kernels  144 us (95%)
  local copies, waits for them, and re-layouts  6.75 us (4%)
    pallas_call x2, Pallas kernels, gather_all(): pl.pallas_call(functools.partial(gather_kernel, parts, count, prologue, l...  79.1 us
    pallas_call x1, Pallas kernels, per_device(): pl.pallas_call(first_kernel, out_shape=[jax.ShapeDtypeStruct((units, BAND...  46.9 us
    pallas_call x1, Pallas kernels, per_device(): pl.pallas_call(second_kernel, out_shape=jax.ShapeDtypeStruct((BANDS, patc...  18.5 us
    unnamed x22, local copies, waits for them, and re-layouts  6.75 us

profile of v3, /device:TPU:1, one launch (start us, length us, event | category | flops | bytes accessed | tf_op | source)
XLA Modules:
  0.0 151.3 jit_solution(6176526899655578550)
XLA Ops:
  0.0 0.0 copy-start
  0.0 0.9 copy-done
  0.9 0.0 copy-start.3
  0.9 0.8 copy-done.3
  1.7 0.0 copy-start.4
  1.7 0.8 copy-done.4
  2.4 0.0 copy-start.8
  2.4 0.7 copy-done.8
  3.1 0.0 copy-start.9
  3.1 0.7 copy-done.9
  3.8 0.0 copy-start.10
  3.8 0.7 copy-done.10
  4.5 47.8 %gather_all.2 = (f32[4,4,4,2,16,8,128]{6,5,4,3,2,1,0:T(8,128)S(1)}, bf16[4,4,4,2,16,16,128]{6,5,4,3,2,1,0:T(8,128)(2,1)S(1)}) custom-call(f32[3,2048]{1,0:T(4,128)S(1)} %copy-done.3, f32[3,2048]{1,0:T(4,128)S(1)} %copy-done.4, f32[16,2048]{1,0:T(8,128)S(1)} %copy-done, s32[1,2048]{1,0:T(1,128)S(1)} %bitcast.13, f32[8]{0:T(128)S(1)} %copy-done.10, ...), custom_call_target="tpu_custom_call" | custom-call | tf_op jit(solution)/shard_map/gather_all/pallas_call | solution.py:211
  52.3 0.0 copy-start.1
  52.3 0.9 copy-done.1
  53.2 0.0 copy-start.5
  53.2 0.7 copy-done.5
  53.9 0.0 copy-start.6
  53.9 0.7 copy-done.6
  54.6 46.9 %first_sweep.1 = (bf16[16,16,128]{2,1,0:T(8,128)(2,1)S(1)}, bf16[344,256,256]{2,1,0:T(8,128)(2,1)}, s32[520]{0:T(1024)S(1)}, s32[1]{0:T(128)}, f32[1024,2,8,128]{3,2,1,0:T(8,128)S(1)}) custom-call(f32[1024,2,8,128]{3,2,1,0:T(8,128)S(1)} %bitcast.9, bf16[1024,2,16,128]{3,2,1,0:T(8,128)(2,1)S(1)} %bitcast.10, f32[16,2048]{1,0:T(8,128)S(1)} %copy-done.1, ...), custom_call_target="tpu_custom_call" | custom-call | tf_op jit(solution)/shard_map/first_sweep/pallas_call | solution.py:531
  101.5 0.0 copy-start.2
  101.5 0.0 copy-start.7
  101.5 31.2 %gather_all.3 = bf16[4,4,4,2,16,16,128]{6,5,4,3,2,1,0:T(8,128)(2,1)S(1)} custom-call(bf16[16,16,128]{2,1,0:T(8,128)(2,1)S(1)} %get-tuple-element.17.refs_0_), custom_call_target="tpu_custom_call" | custom-call | tf_op jit(solution)/shard_map/gather_all/pallas_call | solution.py:211
  132.8 0.0 copy-done.2
  132.8 0.0 copy-done.7
  132.8 18.5 %second_sweep.1 = f32[16,2048]{1,0:T(8,128)} custom-call(s32[520]{0:T(1024)S(1)} %get-tuple-element.14.list_ref, s32[1]{0:T(128)} %get-tuple-element.15.count_ref, f32[1024,2,8,128]{3,2,1,0:T(8,128)S(1)} %get-tuple-element.16.geo_all, bf16[1024,2,16,128]{3,2,1,0:T(8,128)(2,1)S(1)} %bitcast.8, f32[16,2048]{1,0:T(8,128)S(1)} %copy-done.2, ...), custom_call_target="tpu_custom_call" | custom-call | tf_op jit(solution)/shard_map/second_sweep/pallas_call | solution.py:555
Async XLA Ops:
  0.0 0.9 copy-start
  0.9 0.8 copy-start.3
  1.7 0.8 copy-start.4
  2.4 0.7 copy-start.8
  3.1 0.7 copy-start.9
  3.8 0.7 copy-start.10
  52.3 0.9 copy-start.1
  53.2 0.7 copy-start.5
  53.9 0.7 copy-start.6
  101.5 31.3 %copy-start.2 = (f32[16,2048]{1,0:T(8,128)S(1)}, f32[16,2048]{1,0:T(8,128)}, u32[]{:S(2)}) copy-start(f32[16,2048]{1,0:T(8,128)} %emission_ref.3) | copy-start | bytes 393220
  101.5 31.3 %copy-start.7 = (f32[8,16]{1,0:T(8,128)S(1)}, f32[8,16]{1,0:T(8,128)}, u32[]{:S(2)}) copy-start(f32[8,16]{1,0:T(8,128)} %table_ref.3) | copy-start | bytes 1540

commit v4 on v3

--- a/solution.py
+++ b/solution.py
@@ -45,14 +45,21 @@
 
 
 def own_first(refs, srcs):
-    position_ref, normal_ref, emission_ref, level_ref, area_ref, slot_ref = refs
-    geo_ref, flux_ref = srcs
+    geo_ref, flux_ref, *held, load_sem = srcs
+    loads = [
+        pltpu.make_async_copy(ref, to, load_sem.at[n]) for n, (ref, to) in enumerate(zip(refs, held))
+    ]
+    for load in loads:
+        load.start()
+    for load in loads:
+        load.wait()
+    position_ref, normal_ref, emission_ref, level_ref, area_ref, slot_ref = held
     for u in range(position_ref.shape[1] // HALF):
         lanes = slice(u * HALF, (u + 1) * HALF)
         level = level_ref[:, lanes]
         area = jnp.zeros(level.shape, jnp.float32)
-        for m in range(area_ref.shape[0]):
-            area = jnp.where(level == m, area_ref[m], area)
+        for m in range(area_ref.shape[1]):
+            area = jnp.where(level == m, area_ref[0:1, m : m + 1], area)
         code = jnp.zeros(area.shape, jnp.float32)
         if u < 2:
             row, column = slot_ref[u, 0:1, :], slot_ref[u, 1:2, :]
@@ -207,7 +214,10 @@
 def gather_all(shapes, parts, collective_id, specs, inputs, prologue=None):
     count = len(shapes)
     copies = 39 * sum(len(p) for p in parts)
-    own = [pltpu.VMEM(a.shape, a.dtype) for a in shapes] if prologue else []
+    own = []
+    if prologue:
+        own = [pltpu.VMEM(a.shape, a.dtype) for a in list(shapes) + list(inputs)]
+        own.append(pltpu.SemaphoreType.DMA((len(inputs),)))
     return pl.pallas_call(
         functools.partial(gather_kernel, parts, count, prologue, len(inputs)),
         out_shape=[
@@ -320,9 +330,7 @@
         offset = jnp.concatenate([offset, offset], axis=1)
         over = jnp.maximum(facing, 0.0) * jnp.maximum(seen, 0.0)
         under = spread * ((spread - offset) - source_offset)
-        inverse = pl.reciprocal(under, approx=True)
-        inverse = inverse * (2.0 - under * inverse)
-        tile_ref[slot, r : r + CHUNK, :] = (over * inverse).astype(jnp.bfloat16)
+        tile_ref[slot, r : r + CHUNK, :] = (over / under).astype(jnp.bfloat16)
 
 
 def add_product(t, flux, tile, sum_ref):
@@ -339,11 +347,18 @@
 
 
 def first_kernel(
-    geo_ref, flux_ref, emission_ref, material_ref, table_ref,
+    geo_ref, flux_ref, emission_all, material_all, table_all,
     leaving_ref, tiles_ref, list_ref, count_ref, kept_ref,
-    code_ref, entry_ref, slot_ref, slot_sem, centre_ref, column_ref, offset_ref, sum_ref, *rest,
+    emission_ref, material_ref, table_ref, load_sem, code_ref, entry_ref, slot_ref, slot_sem, centre_ref, column_ref, offset_ref, sum_ref, *rest,
 ):
     bufs, sem = rest[:STEP], rest[STEP]
+    loads = [
+        pltpu.make_async_copy(emission_all, emission_ref, load_sem.at[0]),
+        pltpu.make_async_copy(material_all, material_ref, load_sem.at[1]),
+        pltpu.make_async_copy(table_all, table_ref, load_sem.at[2]),
+    ]
+    for load in loads:
+        load.start()
     first = my_block()
     peers = geo_ref.shape[0] // 8
     peer = lax.broadcasted_iota(jnp.int32, (1, peers), 1)
@@ -433,6 +448,8 @@
             for k in range(STEP):
                 out_copy(rounds - back, k).wait()
 
+    for load in loads:
+        load.wait()
     for u in range(16):
         lanes = slice(u * HALF, (u + 1) * HALF)
         reflect = reflect_of(table_ref, material_ref, lanes)
@@ -508,16 +525,18 @@
     vmem = pl.BlockSpec(memory_space=pltpu.VMEM)
     smem = pl.BlockSpec(memory_space=pltpu.SMEM)
     anywhere = pl.BlockSpec(memory_space=pl.ANY)
+    resident = pl.BlockSpec(memory_space=pltpu.HBM)
     material, level = material.reshape(1, patches), area_level.reshape(1, patches)
     slots = jnp.transpose(pair_slots[0], (1, 2, 0))
+    pin = lambda x: pltpu.with_memory_space_constraint(x, pltpu.HBM)
     geo_units = jax.ShapeDtypeStruct((units, 8, HALF), jnp.float32)
     flux_units = jax.ShapeDtypeStruct((units, BANDS, HALF), jnp.bfloat16)
     geo, flux = gather_all(
         [geo_units, flux_units],
         FIRST_PARTS,
         0,
-        [vmem] * 4 + [smem, vmem],
-        [positions, normals, emission, level, area_table, slots],
+        [resident] * 6,
+        [pin(x) for x in (positions, normals, emission, level, area_table.reshape(1, -1), slots)],
         own_first,
     )
     geo = geo.reshape(blocks, 2, 8, HALF)
@@ -537,9 +556,13 @@
             jax.ShapeDtypeStruct((1,), jnp.int32),
             jax.ShapeDtypeStruct(geo.shape, jnp.float32),
         ],
-        in_specs=[vmem] * 5,
+        in_specs=[vmem] * 2 + [resident] * 3,
         out_specs=[vmem, anywhere, smem, smem, anywhere],
         scratch_shapes=[
+            pltpu.VMEM(emission.shape, jnp.float32),
+            pltpu.VMEM(material.shape, jnp.int32),
+            pltpu.VMEM(reflect_table.shape, jnp.float32),
+            pltpu.SemaphoreType.DMA((3,)),
             pltpu.VMEM((peers, HALF), jnp.float32),
             pltpu.VMEM((8, peers), jnp.int32),
             pltpu.SMEM((8, peers), jnp.int32),
@@ -550,7 +573,7 @@
         + [pltpu.SemaphoreType.DMA((2, STEP))],
         compiler_params=pltpu.CompilerParams(vmem_limit_bytes=14 << 20),
         name="first_sweep",
-    )(geo, flux.reshape(blocks, 2, BANDS, HALF), emission, material, reflect_table)
+    )(geo, flux.reshape(blocks, 2, BANDS, HALF), pin(emission), pin(material), pin(reflect_table))
     (flux,) = gather_all([flux_units], LATER_PARTS, 1, [anywhere], [leaving])
     return pl.pallas_call(
         second_kernel,

time: 152 us -> 141 us (0.928)
  local copies, waits for them, and re-layouts: 6.75 us -> 0.02 us
  Pallas kernels: 144 us -> 140 us
    unnamed x22 -> x6, local copies, waits for them, and re-layouts: 6.75 us -> 0.02 us
    pallas_call x1, Pallas kernels: 46.9 us -> 40.9 us  [per_device(): pl.pallas_call(first_kernel, out_shape=[jax.ShapeDtypeStruct((units, BAND...]
    pallas_call x2, Pallas kernels: 79.1 us -> 82.4 us  [gather_all(): pl.pallas_call(functools.partial(gather_kernel, parts, count, prologue, l...]
where the time goes in v4:
time: 141 us
  Pallas kernels  140 us (99%)
    pallas_call x2, Pallas kernels, gather_all(): pl.pallas_call(functools.partial(gather_kernel, parts, count, prologue, l...  82.4 us
    pallas_call x1, Pallas kernels, per_device(): pl.pallas_call(first_kernel, out_shape=[jax.ShapeDtypeStruct((units, BAND...  40.9 us
    pallas_call x1, Pallas kernels, per_device(): pl.pallas_call(second_kernel, out_shape=jax.ShapeDtypeStruct((BANDS, patc...  17.2 us

profile of v4, /device:TPU:1, one launch (start us, length us, event | category | flops | bytes accessed | tf_op | source)
XLA Modules:
  0.0 140.6 jit_solution(15611023101101538414)
XLA Ops:
  0.0 47.3 %gather_all.2 = (f32[4,4,4,2,16,8,128]{6,5,4,3,2,1,0:T(8,128)S(1)}, bf16[4,4,4,2,16,16,128]{6,5,4,3,2,1,0:T(8,128)(2,1)S(1)}) custom-call(f32[3,2048]{1,0:T(4,128)} %refs_0_.1, f32[3,2048]{1,0:T(4,128)} %refs_1_.1, f32[16,2048]{1,0:T(8,128)} %emission_ref.1, s32[1,2048]{1,0:T(1,128)} %bitcast.14, f32[1,8]{1,0:T(1,128)} %bitcast.16, s32[2,2,128]{2,1,0:T(2,128)} %bitcast.15), custom_call_target="tpu_custom_call" | custom-call | tf_op jit(solution)/shard_map/gather_all/pallas_call | solution.py:221
  47.3 40.9 %first_sweep.1 = (bf16[16,16,128]{2,1,0:T(8,128)(2,1)S(1)}, bf16[344,256,256]{2,1,0:T(8,128)(2,1)}, s32[520]{0:T(1024)S(1)}, s32[1]{0:T(128)}, f32[1024,2,8,128]{3,2,1,0:T(8,128)S(1)}) custom-call(f32[1024,2,8,128]{3,2,1,0:T(8,128)S(1)} %bitcast.10, bf16[1024,2,16,128]{3,2,1,0:T(8,128)(2,1)S(1)} %bitcast.11, f32[16,2048]{1,0:T(8,128)} %emission_ref.1, ...), custom_call_target="tpu_custom_call" | custom-call | tf_op jit(solution)/shard_map/first_sweep/pallas_call | solution.py:550
  88.2 0.0 copy-start
  88.2 0.0 copy-start.1
  88.2 0.0 copy-start.2
  88.3 35.1 %gather_all.3 = bf16[4,4,4,2,16,16,128]{6,5,4,3,2,1,0:T(8,128)(2,1)S(1)} custom-call(bf16[16,16,128]{2,1,0:T(8,128)(2,1)S(1)} %get-tuple-element.17.refs_0_), custom_call_target="tpu_custom_call" | custom-call | tf_op jit(solution)/shard_map/gather_all/pallas_call | solution.py:221
  123.4 0.0 copy-done
  123.4 0.0 copy-done.1
  123.4 0.0 copy-done.2
  123.4 17.2 %second_sweep.1 = f32[16,2048]{1,0:T(8,128)} custom-call(s32[520]{0:T(1024)S(1)} %get-tuple-element.14.list_ref, s32[1]{0:T(128)} %get-tuple-element.15.count_ref, f32[1024,2,8,128]{3,2,1,0:T(8,128)S(1)} %get-tuple-element.16.geo_all, bf16[1024,2,16,128]{3,2,1,0:T(8,128)(2,1)S(1)} %bitcast.9, f32[16,2048]{1,0:T(8,128)S(1)} %copy-done, ...), custom_call_target="tpu_custom_call" | custom-call | tf_op jit(solution)/shard_map/second_sweep/pallas_call | solution.py:578
Async XLA Ops:
  88.2 35.2 %copy-start = (f32[16,2048]{1,0:T(8,128)S(1)}, f32[16,2048]{1,0:T(8,128)}, u32[]{:S(2)}) copy-start(f32[16,2048]{1,0:T(8,128)} %emission_ref.1) | copy-start | bytes 393220
  88.2 35.2 %copy-start.1 = (s32[2048]{0:T(1024)S(1)}, s32[2048]{0:T(1024)}, u32[]{:S(2)}) copy-start(s32[2048]{0:T(1024)} %param.11) | copy-start | bytes 24580
  88.2 35.2 %copy-start.2 = (f32[8,16]{1,0:T(8,128)S(1)}, f32[8,16]{1,0:T(8,128)}, u32[]{:S(2)}) copy-start(f32[8,16]{1,0:T(8,128)} %table_ref.1) | copy-start | bytes 1540

commit v5 on v4

--- a/solution.py
+++ b/solution.py
@@ -19,8 +19,8 @@
 FIRST_PARTS = (((0, 11), (1, 5)), ((1, 6), (2, 10)))
 LATER_PARTS = (((0, 6), (1, 5), (2, 5)),)
 KEPT = 336
-STEP = 8
-STEP2 = 8
+STEP = 16
+STEP2 = 16
 CHUNK = 64
 DEPTH = 4
 SKIP = 8 << 10
@@ -202,8 +202,6 @@
             b, k, first, size = item
             for copy in again[item, row]:
                 copy.wait_recv()
-            if row == 1:
-                pass
             share(b, at(k, None, row, 2), first, size)
     for copy in shared:
         copy.wait_recv()
@@ -551,7 +549,7 @@
         first_kernel,
         out_shape=[
             jax.ShapeDtypeStruct((units, BANDS, HALF), jnp.bfloat16),
-            jax.ShapeDtypeStruct((KEPT + 8, BLK, BLK), jnp.bfloat16),
+            jax.ShapeDtypeStruct((KEPT + STEP2, BLK, BLK), jnp.bfloat16),
             jax.ShapeDtypeStruct((4 * peers + STEP2,), jnp.int32),
             jax.ShapeDtypeStruct((1,), jnp.int32),
             jax.ShapeDtypeStruct(geo.shape, jnp.float32),
@@ -571,7 +569,7 @@
         + scratch
         + [pltpu.VMEM((2, BLK, BLK), jnp.bfloat16)] * STEP
         + [pltpu.SemaphoreType.DMA((2, STEP))],
-        compiler_params=pltpu.CompilerParams(vmem_limit_bytes=14 << 20),
+        compiler_params=pltpu.CompilerParams(vmem_limit_bytes=20 << 20),
         name="first_sweep",
     )(geo, flux.reshape(blocks, 2, BANDS, HALF), pin(emission), pin(material), pin(reflect_table))
     (flux,) = gather_all([flux_units], LATER_PARTS, 1, [anywhere], [leaving])
@@ -590,7 +588,7 @@
             pltpu.VMEM((DEPTH, STEP2, BLK, BLK), jnp.bfloat16),
             pltpu.SemaphoreType.DMA((DEPTH,)),
         ],
-        compiler_params=pltpu.CompilerParams(vmem_limit_bytes=22 << 20),
+        compiler_params=pltpu.CompilerParams(vmem_limit_bytes=34 << 20),
         name="second_sweep",
     )(
         listed, counted, kept, flux.reshape(blocks, 2, BANDS, HALF), emission, material,

time: 141 us -> 138 us (0.979)
  Pallas kernels: 140 us -> 137 us
    pallas_call x2, Pallas kernels: 82.4 us -> 77.1 us  [gather_all(): pl.pallas_call(functools.partial(gather_kernel, parts, count, prologue, l...]
    pallas_call x1, Pallas kernels: 40.9 us -> 44.3 us  [per_device(): pl.pallas_call(first_kernel, out_shape=[jax.ShapeDtypeStruct((units, BAND...]
where the time goes in v5:
time: 138 us
  Pallas kernels  137 us (99%)
    pallas_call x2, Pallas kernels, gather_all(): pl.pallas_call(functools.partial(gather_kernel, parts, count, prologue, l...  77.1 us
    pallas_call x1, Pallas kernels, per_device(): pl.pallas_call(first_kernel, out_shape=[jax.ShapeDtypeStruct((units, BAND...  44.3 us
    pallas_call x1, Pallas kernels, per_device(): pl.pallas_call(second_kernel, out_shape=jax.ShapeDtypeStruct((BANDS, patc...  16 us

profile of v5, /device:TPU:1, one launch (start us, length us, event | category | flops | bytes accessed | tf_op | source)
XLA Modules:
  0.0 137.5 jit_solution(15159859863635771739)
XLA Ops:
  0.0 47.3 %gather_all.2 = (f32[4,4,4,2,16,8,128]{6,5,4,3,2,1,0:T(8,128)S(1)}, bf16[4,4,4,2,16,16,128]{6,5,4,3,2,1,0:T(8,128)(2,1)S(1)}) custom-call(f32[3,2048]{1,0:T(4,128)} %refs_0_.1, f32[3,2048]{1,0:T(4,128)} %refs_1_.1, f32[16,2048]{1,0:T(8,128)} %emission_ref.1, s32[1,2048]{1,0:T(1,128)} %bitcast.14, f32[1,8]{1,0:T(1,128)} %bitcast.16, s32[2,2,128]{2,1,0:T(2,128)} %bitcast.15), custom_call_target="tpu_custom_call" | custom-call | tf_op jit(solution)/shard_map/gather_all/pallas_call | solution.py:219
  47.3 44.3 %first_sweep.1 = (bf16[16,16,128]{2,1,0:T(8,128)(2,1)S(1)}, bf16[352,256,256]{2,1,0:T(8,128)(2,1)}, s32[528]{0:T(1024)S(1)}, s32[1]{0:T(128)}, f32[1024,2,8,128]{3,2,1,0:T(8,128)S(1)}) custom-call(f32[1024,2,8,128]{3,2,1,0:T(8,128)S(1)} %bitcast.10, bf16[1024,2,16,128]{3,2,1,0:T(8,128)(2,1)S(1)} %bitcast.11, f32[16,2048]{1,0:T(8,128)} %emission_ref.1, ...), custom_call_target="tpu_custom_call" | custom-call | tf_op jit(solution)/shard_map/first_sweep/pallas_call | solution.py:548
  91.6 0.0 copy-start
  91.6 0.0 copy-start.1
  91.7 0.0 copy-start.2
  91.7 29.8 %gather_all.3 = bf16[4,4,4,2,16,16,128]{6,5,4,3,2,1,0:T(8,128)(2,1)S(1)} custom-call(bf16[16,16,128]{2,1,0:T(8,128)(2,1)S(1)} %get-tuple-element.17.refs_0_), custom_call_target="tpu_custom_call" | custom-call | tf_op jit(solution)/shard_map/gather_all/pallas_call | solution.py:219
  121.5 0.0 copy-done
  121.5 0.0 copy-done.1
  121.5 0.0 copy-done.2
  121.5 16.0 %second_sweep.1 = f32[16,2048]{1,0:T(8,128)} custom-call(s32[528]{0:T(1024)S(1)} %get-tuple-element.14.list_ref, s32[1]{0:T(128)} %get-tuple-element.15.count_ref, f32[1024,2,8,128]{3,2,1,0:T(8,128)S(1)} %get-tuple-element.16.geo_all, bf16[1024,2,16,128]{3,2,1,0:T(8,128)(2,1)S(1)} %bitcast.9, f32[16,2048]{1,0:T(8,128)S(1)} %copy-done, ...), custom_call_target="tpu_custom_call" | custom-call | tf_op jit(solution)/shard_map/second_sweep/pallas_call | solution.py:576
Async XLA Ops:
  91.6 29.8 %copy-start = (f32[16,2048]{1,0:T(8,128)S(1)}, f32[16,2048]{1,0:T(8,128)}, u32[]{:S(2)}) copy-start(f32[16,2048]{1,0:T(8,128)} %emission_ref.1) | copy-start | bytes 393220
  91.6 29.8 %copy-start.1 = (s32[2048]{0:T(1024)S(1)}, s32[2048]{0:T(1024)}, u32[]{:S(2)}) copy-start(s32[2048]{0:T(1024)} %param.11) | copy-start | bytes 24580
  91.7 29.8 %copy-start.2 = (f32[8,16]{1,0:T(8,128)S(1)}, f32[8,16]{1,0:T(8,128)}, u32[]{:S(2)}) copy-start(f32[8,16]{1,0:T(8,128)} %table_ref.1) | copy-start | bytes 1540

commit v6 on v5

--- a/solution.py
+++ b/solution.py
@@ -21,6 +21,7 @@
 KEPT = 336
 STEP = 16
 STEP2 = 16
+TAIL = 4
 CHUNK = 64
 DEPTH = 4
 SKIP = 8 << 10
@@ -70,7 +71,7 @@
         flux_ref[u] = (area * emission_ref[:, lanes]).astype(jnp.bfloat16)
 
 
-def gather_kernel(parts, count, prologue, inputs, *refs):
+def gather_kernel(parts, count, prologue, inputs, short, *refs):
     bufs, rest = refs[inputs : inputs + count], refs[inputs + count :]
     send_sem, recv_sem, local_sem = rest[:3]
     srcs = rest[3:] if prologue else refs[:count]
@@ -152,18 +153,24 @@
         for copy in line[item]:
             copy.wait_recv()
         mine = at(k, None, 0, 0)
-        plane[item] = {by: pass_on(item, 1, by, mine) for by in (1, -1)}
+        steps = (1, -1, 2) if short else (1, -1)
+        plane[item] = {by: pass_on(item, 1, by, mine) for by in steps}
         for by in (1, -1):
             far[item, 0, by] = pass_on(item, 2, by, mine)
         share(b, mine, first, size)
     for item in work:
         b, k, first, size = item
-        plane[item][1].wait_recv()
-        up = pass_on(item, 1, 1, half(k, at(k, None, -1, 0), 0))
-        plane[item][-1].wait_recv()
-        down = pass_on(item, 1, -1, half(k, at(k, None, 1, 0), 1))
-        ahead[item] = [up, down]
+        if short:
+            ahead[item] = [plane[item][2]]
+        else:
+            plane[item][1].wait_recv()
+            up = pass_on(item, 1, 1, half(k, at(k, None, -1, 0), 0))
+            plane[item][-1].wait_recv()
+            down = pass_on(item, 1, -1, half(k, at(k, None, 1, 0), 1))
+            ahead[item] = [up, down]
         for row in (-1, 1):
+            if short:
+                plane[item][-row].wait_recv()
             index = at(k, None, row, 0)
             for by in (1, -1):
                 far[item, row, by] = pass_on(item, 2, by, index)
@@ -172,6 +179,10 @@
     def forward(item, row):
         k = item[1]
         far[item, row, 1].wait_recv()
+        if short and row == 2:
+            far[item, row, -1].wait_recv()
+            again[item, row] = [far[item, row, 2]]
+            return
         up = pass_on(item, 2, 1, half(k, at(k, None, row, -1), 0))
         far[item, row, -1].wait_recv()
         down = pass_on(item, 2, -1, half(k, at(k, None, row, 1), 1))
@@ -190,7 +201,7 @@
         for copy in ahead[item]:
             copy.wait_recv()
         index = at(k, None, 2, 0)
-        for by in (1, -1):
+        for by in (1, -1, 2) if short else (1, -1):
             far[item, 2, by] = pass_on(item, 2, by, index)
         share(b, index, first, size)
     for row in (-1, 1, 2):
@@ -209,7 +220,7 @@
         copy.wait_send()
 
 
-def gather_all(shapes, parts, collective_id, specs, inputs, prologue=None):
+def gather_all(shapes, parts, collective_id, specs, inputs, prologue=None, short=False):
     count = len(shapes)
     copies = 39 * sum(len(p) for p in parts)
     own = []
@@ -217,7 +228,7 @@
         own = [pltpu.VMEM(a.shape, a.dtype) for a in list(shapes) + list(inputs)]
         own.append(pltpu.SemaphoreType.DMA((len(inputs),)))
     return pl.pallas_call(
-        functools.partial(gather_kernel, parts, count, prologue, len(inputs)),
+        functools.partial(gather_kernel, parts, count, prologue, len(inputs), short),
         out_shape=[
             jax.ShapeDtypeStruct((SIDE, SIDE, SIDE, 2) + a.shape, a.dtype) for a in shapes
         ],
@@ -404,7 +415,8 @@
         keep.start()
         keep.wait()
 
-    rounds = pl.cdiv(n, STEP)
+    rounds = lax.div(n, STEP)
+    rest = n - rounds * STEP
 
     def out_copy(i, k):
         side = lax.rem(i, 2)
@@ -439,12 +451,37 @@
     lax.fori_loop(0, rounds, step, 0)
     last = jnp.where(rounds > 0, list_ref[jnp.maximum(rounds * STEP - 1, 0)], SKIP)
     add_tile(last, STEP - 1, lax.rem(rounds + 1, 2))
-    for back in (2, 1):
-
-        @pl.when(rounds >= back)
+
+    @pl.when(rounds >= 2)
+    def _():
+        for k in range(STEP):
+            out_copy(rounds - 2, k).wait()
+
+    side = lax.rem(rounds, 2)
+    for low in range(0, STEP, TAIL):
+
+        @pl.when(rest > low)
         def _():
-            for k in range(STEP):
-                out_copy(rounds - back, k).wait()
+            codes = [list_ref[rounds * STEP + k] for k in range(low, low + TAIL)]
+            for k in range(low, low + TAIL):
+                t, held, b = decode(codes[k - low])
+                build_tile(held, b, geo_ref, centre_ref, column_ref, offset_ref, bufs[k], side)
+                if k > low:
+                    add_tile(codes[k - low - 1], k - 1, side)
+                out_copy(rounds, k).start()
+            add_tile(codes[-1], low + TAIL - 1, side)
+
+    @pl.when(rounds >= 1)
+    def _():
+        for k in range(STEP):
+            out_copy(rounds - 1, k).wait()
+
+    for low in range(0, STEP, TAIL):
+
+        @pl.when(rest > low)
+        def _():
+            for k in range(low, low + TAIL):
+                out_copy(rounds, k).wait()
 
     for load in loads:
         load.wait()
@@ -572,7 +609,9 @@
         compiler_params=pltpu.CompilerParams(vmem_limit_bytes=20 << 20),
         name="first_sweep",
     )(geo, flux.reshape(blocks, 2, BANDS, HALF), pin(emission), pin(material), pin(reflect_table))
-    (flux,) = gather_all([flux_units], LATER_PARTS, 1, [anywhere], [leaving])
+    (flux,) = gather_all(
+        [flux_units], LATER_PARTS, 1, [anywhere], [leaving], short=True
+    )
     return pl.pallas_call(
         second_kernel,
         out_shape=jax.ShapeDtypeStruct((BANDS, patches), jnp.float32),

time: 138 us -> 136 us (0.986)
    pallas_call x1, Pallas kernels: 44.3 us -> 42 us  [per_device(): pl.pallas_call(first_kernel, out_shape=[jax.ShapeDtypeStruct((units, BAND...]
    pallas_call x2, Pallas kernels: 77.1 us -> 78.6 us  [gather_all(): pl.pallas_call(functools.partial(gather_kernel, parts, count, prologue, l...]
where the time goes in v6:
time: 136 us
  Pallas kernels  136 us (100%)
    pallas_call x2, Pallas kernels, gather_all(): pl.pallas_call(functools.partial(gather_kernel, parts, count, prologue, l...  78.6 us
    pallas_call x1, Pallas kernels, per_device(): pl.pallas_call(first_kernel, out_shape=[jax.ShapeDtypeStruct((units, BAND...  42 us
    pallas_call x1, Pallas kernels, per_device(): pl.pallas_call(second_kernel, out_shape=jax.ShapeDtypeStruct((BANDS, patc...  15.3 us

profile of v6, /device:TPU:1, one launch (start us, length us, event | category | flops | bytes accessed | tf_op | source)
XLA Modules:
  0.0 136.0 jit_solution(3016511279034160585)
XLA Ops:
  0.0 47.3 %gather_all.2 = (f32[4,4,4,2,16,8,128]{6,5,4,3,2,1,0:T(8,128)S(1)}, bf16[4,4,4,2,16,16,128]{6,5,4,3,2,1,0:T(8,128)(2,1)S(1)}) custom-call(f32[3,2048]{1,0:T(4,128)} %refs_0_.1, f32[3,2048]{1,0:T(4,128)} %refs_1_.1, f32[16,2048]{1,0:T(8,128)} %emission_ref.1, s32[1,2048]{1,0:T(1,128)} %bitcast.14, f32[1,8]{1,0:T(1,128)} %bitcast.16, s32[2,2,128]{2,1,0:T(2,128)} %bitcast.15), custom_call_target="tpu_custom_call" | custom-call | tf_op jit(solution)/shard_map/gather_all/pallas_call | solution.py:230
  47.3 42.0 %first_sweep.1 = (bf16[16,16,128]{2,1,0:T(8,128)(2,1)S(1)}, bf16[352,256,256]{2,1,0:T(8,128)(2,1)}, s32[528]{0:T(1024)S(1)}, s32[1]{0:T(128)}, f32[1024,2,8,128]{3,2,1,0:T(8,128)S(1)}) custom-call(f32[1024,2,8,128]{3,2,1,0:T(8,128)S(1)} %bitcast.10, bf16[1024,2,16,128]{3,2,1,0:T(8,128)(2,1)S(1)} %bitcast.11, f32[16,2048]{1,0:T(8,128)} %emission_ref.1, ...), custom_call_target="tpu_custom_call" | custom-call | tf_op jit(solution)/shard_map/first_sweep/pallas_call | solution.py:585
  89.3 0.0 copy-start
  89.3 0.0 copy-start.1
  89.3 0.0 copy-start.2
  89.3 31.3 %gather_all.3 = bf16[4,4,4,2,16,16,128]{6,5,4,3,2,1,0:T(8,128)(2,1)S(1)} custom-call(bf16[16,16,128]{2,1,0:T(8,128)(2,1)S(1)} %get-tuple-element.17.refs_0_), custom_call_target="tpu_custom_call" | custom-call | tf_op jit(solution)/shard_map/gather_all/pallas_call | solution.py:230
  120.7 0.0 copy-done
  120.7 0.0 copy-done.1
  120.7 0.0 copy-done.2
  120.7 15.3 %second_sweep.1 = f32[16,2048]{1,0:T(8,128)} custom-call(s32[528]{0:T(1024)S(1)} %get-tuple-element.14.list_ref, s32[1]{0:T(128)} %get-tuple-element.15.count_ref, f32[1024,2,8,128]{3,2,1,0:T(8,128)S(1)} %get-tuple-element.16.geo_all, bf16[1024,2,16,128]{3,2,1,0:T(8,128)(2,1)S(1)} %bitcast.9, f32[16,2048]{1,0:T(8,128)S(1)} %copy-done, ...), custom_call_target="tpu_custom_call" | custom-call | tf_op jit(solution)/shard_map/second_sweep/pallas_call | solution.py:615
Async XLA Ops:
  89.3 31.4 %copy-start = (f32[16,2048]{1,0:T(8,128)S(1)}, f32[16,2048]{1,0:T(8,128)}, u32[]{:S(2)}) copy-start(f32[16,2048]{1,0:T(8,128)} %emission_ref.1) | copy-start | bytes 393220
  89.3 31.4 %copy-start.1 = (s32[2048]{0:T(1024)S(1)}, s32[2048]{0:T(1024)}, u32[]{:S(2)}) copy-start(s32[2048]{0:T(1024)} %param.11) | copy-start | bytes 24580
  89.3 31.4 %copy-start.2 = (f32[8,16]{1,0:T(8,128)S(1)}, f32[8,16]{1,0:T(8,128)}, u32[]{:S(2)}) copy-start(f32[8,16]{1,0:T(8,128)} %table_ref.1) | copy-start | bytes 1540

commit v7 on v6

--- a/solution.py
+++ b/solution.py
@@ -514,6 +514,9 @@
             in_copy(i).start()
 
     sum_ref[...] = jnp.zeros_like(sum_ref)
+    for u in range(16):
+        lanes = slice(u * HALF, (u + 1) * HALF)
+        out_ref[:, lanes] = reflect_of(table_ref, material_ref, lanes)
 
     def step(i, carry):
         @pl.when(i + DEPTH - 1 < rounds)
@@ -546,8 +549,7 @@
 
     for u in range(16):
         lanes = slice(u * HALF, (u + 1) * HALF)
-        reflect = reflect_of(table_ref, material_ref, lanes)
-        out_ref[:, lanes] = emission_ref[:, lanes] + reflect * sum_ref[u // 2, u % 2]
+        out_ref[:, lanes] = emission_ref[:, lanes] + out_ref[:, lanes] * sum_ref[u // 2, u % 2]
 
 
 def per_device(

time: 136 us -> 134 us (0.985)
  Pallas kernels: 136 us -> 134 us
    pallas_call x1, Pallas kernels: 42 us -> 37.9 us  [per_device(): pl.pallas_call(first_kernel, out_shape=[jax.ShapeDtypeStruct((units, BAND...]
    pallas_call x2, Pallas kernels: 78.6 us -> 82.5 us  [gather_all(): pl.pallas_call(functools.partial(gather_kernel, parts, count, prologue, l...]
    pallas_call x1, Pallas kernels: 15.3 us -> 13.6 us  [per_device(): pl.pallas_call(second_kernel, out_shape=jax.ShapeDtypeStruct((BANDS, patc...]
where the time goes in v7:
time: 134 us
  Pallas kernels  134 us (100%)
    pallas_call x2, Pallas kernels, gather_all(): pl.pallas_call(functools.partial(gather_kernel, parts, count, prologue, l...  82.5 us
    pallas_call x1, Pallas kernels, per_device(): pl.pallas_call(first_kernel, out_shape=[jax.ShapeDtypeStruct((units, BAND...  37.9 us
    pallas_call x1, Pallas kernels, per_device(): pl.pallas_call(second_kernel, out_shape=jax.ShapeDtypeStruct((BANDS, patc...  13.6 us

profile of v7, /device:TPU:1, one launch (start us, length us, event | category | flops | bytes accessed | tf_op | source)
XLA Modules:
  0.0 134.0 jit_solution(7125746427192290910)
XLA Ops:
  0.0 47.3 %gather_all.2 = (f32[4,4,4,2,16,8,128]{6,5,4,3,2,1,0:T(8,128)S(1)}, bf16[4,4,4,2,16,16,128]{6,5,4,3,2,1,0:T(8,128)(2,1)S(1)}) custom-call(f32[3,2048]{1,0:T(4,128)} %refs_0_.1, f32[3,2048]{1,0:T(4,128)} %refs_1_.1, f32[16,2048]{1,0:T(8,128)} %emission_ref.1, s32[1,2048]{1,0:T(1,128)} %bitcast.14, f32[1,8]{1,0:T(1,128)} %bitcast.16, s32[2,2,128]{2,1,0:T(2,128)} %bitcast.15), custom_call_target="tpu_custom_call" | custom-call | tf_op jit(solution)/shard_map/gather_all/pallas_call | solution.py:230
  47.3 37.9 %first_sweep.1 = (bf16[16,16,128]{2,1,0:T(8,128)(2,1)S(1)}, bf16[352,256,256]{2,1,0:T(8,128)(2,1)}, s32[528]{0:T(1024)S(1)}, s32[1]{0:T(128)}, f32[1024,2,8,128]{3,2,1,0:T(8,128)S(1)}) custom-call(f32[1024,2,8,128]{3,2,1,0:T(8,128)S(1)} %bitcast.10, bf16[1024,2,16,128]{3,2,1,0:T(8,128)(2,1)S(1)} %bitcast.11, f32[16,2048]{1,0:T(8,128)} %emission_ref.1, ...), custom_call_target="tpu_custom_call" | custom-call | tf_op jit(solution)/shard_map/first_sweep/pallas_call | solution.py:587
  85.2 0.0 copy-start
  85.2 0.0 copy-start.1
  85.2 0.0 copy-start.2
  85.2 35.2 %gather_all.3 = bf16[4,4,4,2,16,16,128]{6,5,4,3,2,1,0:T(8,128)(2,1)S(1)} custom-call(bf16[16,16,128]{2,1,0:T(8,128)(2,1)S(1)} %get-tuple-element.17.refs_0_), custom_call_target="tpu_custom_call" | custom-call | tf_op jit(solution)/shard_map/gather_all/pallas_call | solution.py:230
  120.4 0.0 copy-done
  120.4 0.0 copy-done.1
  120.4 0.0 copy-done.2
  120.4 13.6 %second_sweep.1 = f32[16,2048]{1,0:T(8,128)} custom-call(s32[528]{0:T(1024)S(1)} %get-tuple-element.14.list_ref, s32[1]{0:T(128)} %get-tuple-element.15.count_ref, f32[1024,2,8,128]{3,2,1,0:T(8,128)S(1)} %get-tuple-element.16.geo_all, bf16[1024,2,16,128]{3,2,1,0:T(8,128)(2,1)S(1)} %bitcast.9, f32[16,2048]{1,0:T(8,128)S(1)} %copy-done, ...), custom_call_target="tpu_custom_call" | custom-call | tf_op jit(solution)/shard_map/second_sweep/pallas_call | solution.py:617
Async XLA Ops:
  85.2 35.2 %copy-start = (f32[16,2048]{1,0:T(8,128)S(1)}, f32[16,2048]{1,0:T(8,128)}, u32[]{:S(2)}) copy-start(f32[16,2048]{1,0:T(8,128)} %emission_ref.1) | copy-start | bytes 393220
  85.2 35.2 %copy-start.1 = (s32[2048]{0:T(1024)S(1)}, s32[2048]{0:T(1024)}, u32[]{:S(2)}) copy-start(s32[2048]{0:T(1024)} %param.11) | copy-start | bytes 24580
  85.2 35.2 %copy-start.2 = (f32[8,16]{1,0:T(8,128)S(1)}, f32[8,16]{1,0:T(8,128)}, u32[]{:S(2)}) copy-start(f32[8,16]{1,0:T(8,128)} %table_ref.1) | copy-start | bytes 1540
